TPU v7x, 128 devices: a whole 4x4x4 slice. The times are simulated.
128 devices in a mesh: grp: 2 (over y_lo), seq: 32 (over x, z, core), dp: 2 (over y_hi).
Axes of the slice: x: 4, y: 4 (y_hi: 2, y_lo: 2; y = y_hi * 2 + y_lo), z: 4, core: 2. Of those that a mesh axis runs over, the one named last changes fastest.
Arguments:
- counts: int32 [2, 32, 2, 256, 1024], P('dp', 'seq', 'grp'), may hold values from 0 to 23
- valid_frames: int32 [2, 4], replicated, may hold values from 2 to 16, as said below
- cotangent: bfloat16 [2, 64, 256, 1024], P('dp', 'seq'), may hold values from -0.125 to 0.125
- pillar_proj: bfloat16 [1024, 1024], replicated, may hold values from -0.1875 to 0.1875
- pillar_gain: float32 [1024], replicated, may hold values from 0.1 to 1.9
- latent_proj: bfloat16 [1024, 1024], replicated, may hold values from -0.1875 to 0.1875
- input_proj: bfloat16 [1024, 1024], replicated, may hold values from -0.1875 to 0.1875
- space_gain: float32 [1024], replicated, may hold values from 0.1 to 1.9
- space_project: bfloat16 [1024, 3072], replicated, may hold values from -0.1875 to 0.1875
- space_output: bfloat16 [1024, 1024], replicated, may hold values from -0.1875 to 0.1875
- time_gain: float32 [1024], replicated, may hold values from 0.1 to 1.9
- time_project: bfloat16 [1024, 3072], replicated, may hold values from -0.1875 to 0.1875
- time_output: bfloat16 [1024, 1024], replicated, may hold values from -0.75 to 0.75
Outputs:
- pillar_grad: float32 [1024, 1024], P(('grp', 'seq', 'dp'))
- latent_grad: float32 [1024, 1024], P(('grp', 'seq', 'dp'))
Inputs may be any that keep to these rules, and one draw needn't show every extreme that they name: `valid_frames`: exactly one scene has all 16 frames valid.
All inputs are finite; a program needn't handle non-finite values.
Results may differ from a plain program's by a relative error of at most 0.0095.
Values may be sent and summed in bfloat16 or wider, within the bound.
No kernel may reach another device: no remote copies, remote signals or barrier semaphores. Data moves between devices by JAX's collectives and lax.ppermute only.
A program may use at most 128 MiB of HBM per device.

v0:
```python
import jax
import jax.numpy as jnp
from jax import lax
from jax.sharding import PartitionSpec as P

HEADS = 8
FRAMES = 16


def scaled_norm(values, norm_gain):
    return values * lax.rsqrt(jnp.mean(values * values, axis=-1, keepdims=True) + 1e-06) * norm_gain


def head_norm(values):
    values = values.astype(jnp.float32)
    return (values * lax.rsqrt(jnp.mean(values * values, axis=-1, keepdims=True) + 1e-06)).astype(
        jnp.bfloat16
    )


def project(activations, weight):
    return jnp.dot(activations, weight, preferred_element_type=jnp.float32)


def split_heads(joined, head_count):
    shaped = joined.reshape(
        joined.shape[:-1] + (3, head_count, joined.shape[-1] // (3 * head_count))
    )
    return (head_norm(shaped[..., 0, :, :]), head_norm(shaped[..., 1, :, :]), shaped[..., 2, :, :])


def space_core(joined, head_count):
    queries, keys, values = split_heads(joined, head_count)
    score_scale = queries.shape[-1] ** (-0.5)
    scores = (
        jnp.einsum("grphd,grqhd->grhpq", queries, keys, preferred_element_type=jnp.float32)
        * score_scale
    )
    weights = jnp.exp(scores)
    weights = (weights / jnp.sum(weights, axis=-1, keepdims=True)).astype(jnp.bfloat16)
    mixture = jnp.einsum("grhpq,grqhd->grphd", weights, values, preferred_element_type=jnp.float32)
    return mixture.astype(jnp.bfloat16).reshape(joined.shape[:-1] + (-1,))


def time_core(joined, head_count, visible):
    queries, keys, values = split_heads(joined, head_count)
    score_scale = queries.shape[-1] ** (-0.5)
    scores = (
        jnp.einsum("gsfthd,gsethd->gsthfe", queries, keys, preferred_element_type=jnp.float32)
        * score_scale
    )
    weights = jnp.exp(scores) * visible
    weights = (weights / jnp.sum(weights, axis=-1, keepdims=True)).astype(jnp.bfloat16)
    mixture = jnp.einsum(
        "gsthfe,gsethd->gsfthd", weights, values, preferred_element_type=jnp.float32
    )
    return mixture.astype(jnp.bfloat16).reshape(joined.shape[:-1] + (-1,))


def mixer_inputs(residual, norm_gain, weight):
    return project(scaled_norm(residual, norm_gain).astype(jnp.bfloat16), weight).astype(
        jnp.bfloat16
    )


def space_layer(stream, norm_gain, weight_in, weight_out, head_count):
    residual = stream.astype(jnp.float32)
    joined = mixer_inputs(residual, norm_gain, weight_in)
    return (residual + project(space_core(joined, head_count), weight_out)).astype(jnp.bfloat16)


def visibility(valid_rows, frame_count):
    position = jnp.arange(frame_count, dtype=jnp.int32)
    causal = position[None, :] <= position[:, None]
    allowed = causal[None, None] & (position[None, None, None, :] < valid_rows[:, :, None, None])
    return allowed.astype(jnp.float32)[:, :, None, None]


def activation(inputs, norm_gain):
    return jax.nn.gelu(scaled_norm(inputs, norm_gain))


def frame_order(values):
    count = values.shape[1]
    shaped = values.reshape((1, 2, count // 2) + values.shape[2:])
    return jnp.swapaxes(shaped, 1, 2).reshape(values.shape)


def side_order(values):
    count = values.shape[1]
    shaped = values.reshape((1, count // 2, 2) + values.shape[2:])
    return jnp.swapaxes(shaped, 1, 2).reshape(values.shape)


def shards(
    counts,
    valid_frames,
    cotangent,
    pillar_proj,
    pillar_gain,
    latent_proj,
    input_proj,
    space_gain,
    space_project,
    space_output,
    time_gain,
    time_project,
    time_output,
):
    group_side = lax.axis_index("grp")
    features = jnp.log1p(counts.astype(jnp.float32)).astype(jnp.bfloat16)
    features = features.reshape(1, 1, features.shape[3], features.shape[4])

    def tokenize(pillars):
        before = project(pillars, pillar_proj)
        hidden, activation_back = jax.vjp(lambda inputs: activation(inputs, pillar_gain), before)
        hidden = hidden.astype(jnp.bfloat16)
        return (project(hidden, latent_proj).astype(jnp.bfloat16), hidden, activation_back)

    latents, hidden, activation_back = tokenize(features)
    pillars = features
    own_cot = lax.dynamic_slice_in_dim(cotangent, group_side, 1, 1)

    def front_part(latent_in):
        stream = project(latent_in, input_proj).astype(jnp.bfloat16)
        return space_layer(stream, space_gain, space_project, space_output, HEADS)

    spatial_out, front_back = jax.vjp(front_part, latents)
    scenes = valid_frames.shape[1]
    visible = visibility(lax.dynamic_slice_in_dim(valid_frames, lax.axis_index("dp"), 1, 0), FRAMES)
    residual = spatial_out.astype(jnp.float32)
    joined, inputs_back = jax.vjp(
        lambda stream: mixer_inputs(stream, time_gain, time_project), residual
    )
    mixture_grad = jnp.einsum(
        "grpd,id->grpi", own_cot, time_output, preferred_element_type=jnp.float32
    ).astype(jnp.bfloat16)
    tile_joined = frame_order(
        lax.all_to_all(joined, ("grp", "seq"), split_axis=2, concat_axis=1, tiled=True)
    )
    tile_mixture_grad = frame_order(
        lax.all_to_all(mixture_grad, ("grp", "seq"), split_axis=2, concat_axis=1, tiled=True)
    )
    tile_count = tile_joined.shape[2]

    def core_step(stream):
        mixed_tiles = time_core(stream.reshape(1, scenes, FRAMES, tile_count, -1), HEADS, visible)
        return mixed_tiles.reshape(stream.shape[:-1] + (-1,))

    unused, core_back = jax.vjp(core_step, tile_joined)
    joined_tile_grad = core_back(tile_mixture_grad)[0]
    joined_grad = lax.all_to_all(
        side_order(joined_tile_grad), ("grp", "seq"), split_axis=1, concat_axis=2, tiled=True
    )
    spatial_grad = (own_cot.astype(jnp.float32) + inputs_back(joined_grad)[0]).astype(jnp.bfloat16)
    stream_grad = front_back(spatial_grad)[0]
    kept_share = jnp.float32(1.0)
    hidden_flat = hidden.reshape(-1, hidden.shape[-1])
    grad_flat = stream_grad.reshape(-1, stream_grad.shape[-1])
    latent_part = (
        jnp.einsum("th,tl->hl", hidden_flat, grad_flat, preferred_element_type=jnp.float32)
        * kept_share
    )
    hidden_grad = jnp.einsum(
        "grpl,hl->grph", stream_grad, latent_proj, preferred_element_type=jnp.float32
    )
    before_grad = activation_back(hidden_grad)[0].astype(jnp.bfloat16)
    pillar_flat = pillars.reshape(-1, pillars.shape[-1])
    before_flat = before_grad.reshape(-1, before_grad.shape[-1])
    pillar_part = (
        jnp.einsum("tp,th->ph", pillar_flat, before_flat, preferred_element_type=jnp.float32)
        * kept_share
    )
    return (
        lax.psum_scatter(pillar_part, ("grp", "seq", "dp"), scatter_dimension=0, tiled=True),
        lax.psum_scatter(latent_part, ("grp", "seq", "dp"), scatter_dimension=0, tiled=True),
    )


def solution(mesh):
    placed = (
        P("dp", "seq", "grp", None, None),
        P(),
        P("dp", "seq", None, None),
        P(),
        P(),
        P(),
        P(),
        P(),
        P(),
        P(),
        P(),
        P(),
        P(),
    )
    return jax.shard_map(
        shards,
        mesh=mesh,
        in_specs=placed,
        out_specs=(P(("grp", "seq", "dp"), None), P(("grp", "seq", "dp"), None)),
        check_vma=False,
    )
```

profile of v0, /device:TPU:0, one launch (start us, length us, event | category | flops | bytes accessed | tf_op | source)
XLA Modules:
  0.0 1523.8 jit_solution(11691434853554041101)
XLA Ops:
  11.2 4.5 reduce.33
  17.8 10.2 all-to-all-start
  30.9 4.2 fusion.81
  35.1 6.0 convolution_convert_fusion.1
  53.5 4.1 copy.182
  57.6 12.8 reduce.32
  70.4 4.6 reshape.737
  75.0 9.2 all-to-all-start.1
  88.0 3.8 bitcast_reduce_fusion.1
  93.6 13.6 all-to-all-done.1
  107.2 10.5 reshape.738
  117.8 12.2 bitcast_reduce_fusion
  130.0 3.9 reshape.711
  137.2 4.0 reshape_reshape.8
  151.3 4.0 reshape.713
  159.9 5.5 all-to-all-start.2
  165.5 22.9 %all-to-all-done.2 = bf16[1,64,4,3072]{3,2,0,1:T(4,128)(2,1)} async-done(((bf16[1,64,4,3072]{3,2,0,1:T(4,128)(2,1)}), bf16[1,64,4,3072]{3,2,0,1:T(4,128)(2,1)}, u32[]{:S(2)}, u32[]{:S(2)}) %all-to-all-start.2) | async-done | bytes 1572896 | tf_op jit(solution)/shard_map/all_to_all | solution.py:152
  188.5 3.9 reshape.715
  192.4 5.3 fusion.80
  211.5 3.8 convolution_bitcast_fusion
  215.3 5.3 copy.128
  220.7 4.0 fusion.145
  224.8 644.2 %reduce-scatter.7.cloned.1.call-done = f32[8,1024]{1,0:T(8,128)} async-done(((f32[1024,1024]{1,0:T(8,128)}), f32[8,1024]{1,0:T(8,128)}) %reduce-scatter.7.cloned.1.call-update) | async-done | bytes 32784
  869.0 647.6 %reduce-scatter.5.cloned.1.call-done = f32[8,1024]{1,0:T(8,128)} async-done(((f32[1024,1024]{1,0:T(8,128)}), f32[8,1024]{1,0:T(8,128)}) %reduce-scatter.5.cloned.1.call-update) | async-done | bytes 32784 | tf_op jit(solution)/shard_map/reduce_scatter | solution.py:176
  (122 shorter events, 58.5 us)
Async XLA Ops:
  7.2 23.7 %copy-start = (bf16[1024,1024]{1,0:T(8,128)(2,1)S(1)}, bf16[1024,1024]{1,0:T(8,128)(2,1)}, u32[]{:S(2)}) copy-start(bf16[1024,1024]{1,0:T(8,128)(2,1)} %param.18) | copy-start | bytes 6291460
  17.8 57.2 %all-to-all-start = ((bf16[64,2,2048]{2,1,0:T(2,128)(2,1)}), bf16[64,2,2048]{2,1,0:T(2,128)(2,1)}, u32[]{:S(2)}, u32[]{:S(2)}) async-start(bf16[64,2,2048]{2,1,0:T(2,128)(2,1)} %reshape.739), calls=%async_computation | async-start | bytes 1048576 | tf_op jit(solution)/shard_map/all_to_all | solution.py:142
  28.0 2.9 copy-start.17
  30.8 4.3 copy-start.2
  30.9 4.2 copy-start.20
  45.4 6.2 slice-start
  47.3 2.0 copy-start.6
  47.4 2.5 copy-start.4
  47.4 2.6 copy-start.13
  47.4 4.2 slice-start.1
  49.3 2.3 copy-start.19
  75.0 9.2 copy-start.21
  75.0 32.2 %all-to-all-start.1 = ((bf16[64,2,6144]{2,1,0:T(2,128)(2,1)}), bf16[64,2,6144]{2,1,0:T(2,128)(2,1)}, u32[]{:S(2)}, u32[]{:S(2)}) async-start(bf16[64,2,6144]{2,1,0:T(2,128)(2,1)} %reshape.737), calls=%async_computation.1 | async-start | bytes 3145728 | tf_op jit(solution)/shard_map/all_to_all | solution.py:139
  159.9 28.5 %all-to-all-start.2 = ((bf16[1,64,4,3072]{3,2,0,1:T(4,128)(2,1)}), bf16[1,64,4,3072]{3,2,0,1:T(4,128)(2,1)}, u32[]{:S(2)}, u32[]{:S(2)}) async-start(bf16[1,64,4,3072]{3,2,0,1:T(4,128)(2,1)} %copy.112), calls=%async_computation.2 | async-start | bytes 3145728 | tf_op jit(solution)/shard_map/all_to_all | solution.py:152
  165.4 27.0 %copy-start.9 = (bf16[256,1024]{1,0:T(8,128)(2,1)S(1)}, bf16[256,1024]{1,0:T(8,128)(2,1)}, u32[]{:S(2)}) copy-start(bf16[256,1024]{1,0:T(8,128)(2,1)} %copy-done.8) | copy-start | bytes 1572868
  165.5 703.5 %reduce-scatter.7.cloned.1.call-start = ((), (), s32[]{:S(2)}) async-start(), calls=%async_computation.6 | async-start | bytes 4227072
  192.4 5.3 copy-start.16
  200.4 2.3 copy-start.1
  200.5 2.7 copy-start.7
  203.7 2.2 slice-start.2
  204.3 2.4 slice-start.3
  206.8 2.0 copy-start.12
  206.9 2.0 copy-start.18
  220.7 1295.9 %reduce-scatter.5.cloned.1.call-start = ((), (), s32[]{:S(2)}) async-start(), calls=%async_computation.5 | async-start | bytes 4227072 | tf_op jit(solution)/shard_map/reduce_scatter | solution.py:176
  (7 other events, 8.7 us)
Sparse Core Ops, SparseCore 0:
  220.8 648.1 reduce-scatter.6
  871.9 644.6 reduce-scatter.4
where the time goes:
time: 1530 us; the launch traced here: 1520 us
  waiting for transfers between devices  1330 us (87%)
  local copies, waits for them, and re-layouts  84.2 us (6%)
  matrix products  48.9 us (3%)
  starting transfers between devices  25 us (2%)
  other arithmetic  22.2 us (1%)
    reduce_scatter x1, waiting for transfers between devices, shards(): lax.psum_scatter(latent_part, ('grp', 'seq', 'dp'), scatter_dimension=0,...  648 us
    unnamed x3, waiting for transfers between devices  644 us
    unnamed x58, local copies, waits for them, and re-layouts  31.5 us
  transfers between devices with their start and end apart: 5, of which 4 were waited for; matrix products, arithmetic and copies ran while one was open for 4% of the time, Pallas kernels for 0%

commit v1 on v0

v1 whole, which is shorter than its diff:
```python
import jax
import jax.numpy as jnp
from jax import lax
from jax.experimental import pallas as pl
from jax.experimental.pallas import tpu as pltpu
from jax.sharding import Mesh, PartitionSpec as P

HEADS = 8
HEAD = 128
FRAMES = 16
TOK = 256
D = 1024
EPS = 1e-06
F32 = jnp.float32
BF16 = jnp.bfloat16
SCALE = HEAD**-0.5
VMEM = pl.BlockSpec(memory_space=pltpu.VMEM)
SMEM = pl.BlockSpec(memory_space=pltpu.SMEM)
ANY = pl.BlockSpec(memory_space=pl.ANY)


def dot(a, b):
    return lax.dot_general(a, b, (((1,), (0,)), ((), ())), preferred_element_type=F32)


def dot_nt(a, b):
    return lax.dot_general(a, b, (((1,), (1,)), ((), ())), preferred_element_type=F32)


def dot_tn(a, b):
    return lax.dot_general(a, b, (((0,), (0,)), ((), ())), preferred_element_type=F32)


def inverse_rms(values):
    return lax.rsqrt(jnp.mean(values * values, axis=-1, keepdims=True) + EPS)


def norm_back(values, inverse, grad):
    inner = jnp.mean(values * grad, axis=-1, keepdims=True)
    return inverse * grad - values * (inverse * inverse * inverse * inner)


GELU_A = 0.7978845608028654
GELU_B = 0.044715


def fetch(pairs, sems):
    copies = [
        pltpu.make_async_copy(src, dst, sems.at[k]) for k, (src, dst) in enumerate(pairs)
    ]
    for copy in copies:
        copy.start()
    return copies


def head_parts(j_ref, h):
    q = j_ref[:, pl.ds(pl.multiple_of(h * HEAD, HEAD), HEAD)].astype(F32)
    k = j_ref[:, pl.ds(pl.multiple_of(D + h * HEAD, HEAD), HEAD)].astype(F32)
    v = j_ref[:, pl.ds(pl.multiple_of(2 * D + h * HEAD, HEAD), HEAD)]
    iq = inverse_rms(q)
    ik = inverse_rms(k)
    return q, k, v, iq, ik, (q * iq).astype(BF16), (k * ik).astype(BF16)


def softmax(qn, kn, mask):
    w = jnp.exp(dot_nt(qn, kn) * SCALE)
    if mask is not None:
        w = w * mask
    return w / jnp.sum(w, axis=-1, keepdims=True)


def attention_back(j_ref, dm_ref, dj_ref, mask, h):
    q, k, v, iq, ik, qn, kn = head_parts(j_ref, h)
    weights = softmax(qn, kn, mask)
    cols = pl.ds(pl.multiple_of(h * HEAD, HEAD), HEAD)
    dm = dm_ref[:, cols]
    dp = dot_nt(dm, v).astype(BF16).astype(F32)
    dv = dot_tn(weights.astype(BF16), dm)
    ds = weights * (dp - jnp.sum(dp * weights, axis=-1, keepdims=True)) * SCALE
    ds = ds.astype(BF16)
    dqn = dot(ds, kn).astype(BF16).astype(F32)
    dkn = dot_tn(ds, qn).astype(BF16).astype(F32)
    dj_ref[:, cols] = norm_back(q, iq, dqn).astype(BF16)
    dj_ref[:, pl.ds(pl.multiple_of(D + h * HEAD, HEAD), HEAD)] = norm_back(k, ik, dkn).astype(BF16)
    dj_ref[:, pl.ds(pl.multiple_of(2 * D + h * HEAD, HEAD), HEAD)] = dv.astype(BF16)


def front_kernel(
    counts, pillar_proj, pillar_gain, latent_proj, input_proj, space_gain, space_project,
    space_output, features, before, hidden, stream, joined, spaced,
    w_pillar, w_latent, w_input, w_project, w_output, mixed, sems,
):
    copies = fetch(
        [
            (pillar_proj, w_pillar),
            (latent_proj, w_latent),
            (input_proj, w_input),
            (space_project, w_project),
            (space_output, w_output),
        ],
        sems,
    )
    x = jnp.log(counts[...].astype(F32) + 1.0).astype(BF16)
    features[...] = x
    copies[0].wait()
    b = dot(x, w_pillar[...])
    before[...] = b
    n = b * inverse_rms(b) * pillar_gain[...]
    hid = (0.5 * n * (1.0 + jnp.tanh(GELU_A * (n + GELU_B * n * n * n)))).astype(BF16)
    hidden[...] = hid
    copies[1].wait()
    lat = dot(hid, w_latent[...]).astype(BF16)
    copies[2].wait()
    s = dot(lat, w_input[...]).astype(BF16)
    stream[...] = s
    s = s.astype(F32)
    u = (s * inverse_rms(s) * space_gain[...]).astype(BF16)
    copies[3].wait()
    for part in range(3):
        cols = slice(part * D, (part + 1) * D)
        joined[:, cols] = dot(u, w_project[:, cols]).astype(BF16)

    def head(h, carry):
        q, k, v, iq, ik, qn, kn = head_parts(joined, h)
        weights = softmax(qn, kn, None).astype(BF16)
        mixed[:, pl.ds(pl.multiple_of(h * HEAD, HEAD), HEAD)] = dot(weights, v).astype(BF16)
        return carry

    lax.fori_loop(0, HEADS, head, 0)
    copies[4].wait()
    spaced[...] = (stream[...].astype(F32) + dot(mixed[...], w_output[...])).astype(BF16)


def turn_kernel(features, hidden, feat_own, feat_send, hid_own, hid_send, turned):
    core = lax.axis_index("core")
    for src, own, send in ((features, feat_own, feat_send), (hidden, hid_own, hid_send)):
        turned[...] = src[...].T.reshape(32, 2, 16, TOK)
        own[...] = turned[:, core].reshape(512, TOK)
        send[...] = turned[:, 1 - core].reshape(512, TOK)


def mixture_kernel(cot, time_output, out):
    out[...] = dot_nt(cot[...], time_output[...]).astype(BF16)


def time_kernel(
    valid_frames, spaced, cot, dmixed, time_gain, time_project, grad,
    w_project, joined, djoined, masked, sems,
):
    copies = fetch([(time_project, w_project)], sems)
    valid = valid_frames[lax.axis_index("dp"), lax.axis_index("x")]
    row = lax.broadcasted_iota(jnp.int32, (TOK, TOK), 0)
    col = lax.broadcasted_iota(jnp.int32, (TOK, TOK), 1)
    e = col // FRAMES
    seen = (row % FRAMES == col % FRAMES) & (e <= row // FRAMES) & (e < valid)
    masked[...] = seen.astype(F32)
    s = spaced[...].astype(F32)
    inverse = inverse_rms(s)
    u = (s * inverse * time_gain[...]).astype(BF16)
    copies[0].wait()
    for part in range(3):
        cols = slice(part * D, (part + 1) * D)
        joined[:, cols] = dot(u, w_project[:, cols]).astype(BF16)

    def head(h, carry):
        attention_back(joined, dmixed, djoined, masked[...], h)
        return carry

    lax.fori_loop(0, HEADS, head, 0)
    du = dot_nt(djoined[...], w_project[...]).astype(BF16).astype(F32) * time_gain[...]
    s = spaced[...].astype(F32)
    grad[...] = (cot[...].astype(F32) + norm_back(s, inverse_rms(s), du)).astype(BF16)


def back_kernel(
    dspaced, joined, stream, space_gain, space_output, space_project, input_proj, dlatent,
    w_output, w_project, w_input, dmixed, djoined, sems,
):
    copies = fetch(
        [(space_output, w_output), (space_project, w_project), (input_proj, w_input)], sems
    )
    copies[0].wait()
    dmixed[...] = dot_nt(dspaced[...], w_output[...]).astype(BF16)

    def head(h, carry):
        attention_back(joined, dmixed, djoined, None, h)
        return carry

    lax.fori_loop(0, HEADS, head, 0)
    copies[1].wait()
    du = dot_nt(djoined[...], w_project[...]).astype(BF16).astype(F32) * space_gain[...]
    s = stream[...].astype(F32)
    dstream = (dspaced[...].astype(F32) + norm_back(s, inverse_rms(s), du)).astype(BF16)
    copies[2].wait()
    dlatent[...] = dot_nt(dstream, w_input[...]).astype(BF16)


def token_kernel(dlatent, before, pillar_gain, latent_proj, dbefore):
    dhid = dot_nt(dlatent[...], latent_proj[...])
    b = before[...]
    inverse = inverse_rms(b)
    n = b * inverse * pillar_gain[...]
    t = jnp.tanh(GELU_A * (n + GELU_B * n * n * n))
    slope = 0.5 * (1.0 + t) + 0.5 * n * (1.0 - t * t) * (GELU_A * (1.0 + 3.0 * GELU_B * n * n))
    dn = dhid * slope * pillar_gain[...]
    dbefore[...] = norm_back(b, inverse, dn).astype(BF16)


def weight_kernel(own, other, grad_own, grad_other, out):
    out[...] = (dot(own[...], grad_own[...]) + dot(other[...], grad_other[...])).astype(BF16)


def total_kernel(a, b, out_a, out_b):
    for src, out in ((a, out_a), (b, out_b)):
        out[...] = jnp.sum(src[...].astype(F32).reshape(64, 8, D), axis=0)


def struct(shape, dtype):
    return jax.ShapeDtypeStruct(shape, dtype)


def call(kernel, name, outs, in_specs, args, scratch=(), flops=0, bytes_accessed=0, limit=None):
    many = isinstance(outs, tuple)
    return pl.pallas_call(
        kernel,
        out_shape=outs,
        in_specs=in_specs,
        out_specs=tuple(VMEM for _ in outs) if many else VMEM,
        scratch_shapes=list(scratch),
        name=name,
        cost_estimate=pl.CostEstimate(
            flops=flops, bytes_accessed=bytes_accessed, transcendentals=0
        ),
        compiler_params=pltpu.CompilerParams(vmem_limit_bytes=limit),
    )(*args)


UNIT = 2 * TOK * D * D
MIB = 1 << 20


def shards(
    counts,
    valid_frames,
    cotangent,
    pillar_proj,
    pillar_gain,
    latent_proj,
    input_proj,
    space_gain,
    space_project,
    space_output,
    time_gain,
    time_project,
    time_output,
):
    rows = struct((TOK, D), BF16)
    scene = ("z", "core", "grp")
    rest = ("grp", "x", "z", "dp")
    swap = ((0, 1), (1, 0))
    pillar_gain = pillar_gain.reshape(1, D)
    space_gain = space_gain.reshape(1, D)
    time_gain = time_gain.reshape(1, D)

    def exchange(values, axes):
        return lax.all_to_all(values, axes, split_axis=0, concat_axis=0, tiled=True)

    own_cot = lax.dynamic_index_in_dim(cotangent[0], lax.axis_index("grp"), 0, keepdims=False)
    cot = exchange(own_cot, scene)

    wide = lambda n: pltpu.VMEM((D, n * D), BF16)
    features, before, hidden, stream, joined, spaced = call(
        front_kernel,
        "front",
        (rows, struct((TOK, D), F32), rows, rows, struct((TOK, 3 * D), BF16), rows),
        [VMEM, ANY, VMEM, ANY, ANY, VMEM, ANY, ANY],
        (
            counts.reshape(TOK, D), pillar_proj, pillar_gain, latent_proj, input_proj,
            space_gain, space_project, space_output,
        ),
        [wide(1), wide(1), wide(1), wide(3), wide(1), pltpu.VMEM((TOK, D), BF16),
         pltpu.SemaphoreType.DMA((5,))],
        8 * UNIT,
        20 * MIB,
    )
    half = struct((512, TOK), BF16)
    spaced_tok = exchange(spaced, scene)
    feat_own, feat_send, hid_own, hid_send = call(
        turn_kernel,
        "turn",
        (half, half, half, half),
        [VMEM, VMEM],
        (features, hidden),
        [pltpu.VMEM((32, 2, 16, TOK), BF16)],
        0,
        2 * MIB,
    )
    feat_other = lax.ppermute(feat_send, "core", swap)
    hid_other = lax.ppermute(hid_send, "core", swap)
    dmixed = call(mixture_kernel, "mixture", rows, [VMEM, VMEM], (cot, time_output), (), UNIT, 3 * MIB)
    grad_tok = call(
        time_kernel,
        "time",
        rows,
        [SMEM, VMEM, VMEM, VMEM, VMEM, ANY],
        (valid_frames, spaced_tok, cot, dmixed, time_gain, time_project),
        [wide(3), pltpu.VMEM((TOK, 3 * D), BF16), pltpu.VMEM((TOK, 3 * D), BF16),
         pltpu.VMEM((TOK, TOK), F32), pltpu.SemaphoreType.DMA((1,))],
        8 * UNIT,
        10 * MIB,
    )
    dspaced = exchange(grad_tok, scene)
    dlatent = call(
        back_kernel,
        "back",
        rows,
        [VMEM, VMEM, VMEM, VMEM, ANY, ANY, ANY],
        (dspaced, joined, stream, space_gain, space_output, space_project, input_proj),
        [wide(1), wide(3), wide(1), pltpu.VMEM((TOK, D), BF16), pltpu.VMEM((TOK, 3 * D), BF16),
         pltpu.SemaphoreType.DMA((3,))],
        7 * UNIT,
        14 * MIB,
    )
    dlatent_other = lax.ppermute(dlatent, "core", swap)
    dbefore = call(
        token_kernel,
        "token",
        rows,
        [VMEM, VMEM, VMEM, VMEM],
        (dlatent, before, pillar_gain, latent_proj),
        (),
        UNIT,
        4 * MIB,
    )
    dbefore_other = lax.ppermute(dbefore, "core", swap)
    partial = struct((512, D), BF16)
    latent_part = call(
        weight_kernel, "latent_weight", partial, [VMEM] * 4,
        (hid_own, hid_other, dlatent, dlatent_other), (), UNIT, 2 * MIB,
    )
    latent_parts = exchange(latent_part, rest)
    pillar_part = call(
        weight_kernel, "pillar_weight", partial, [VMEM] * 4,
        (feat_own, feat_other, dbefore, dbefore_other), (), UNIT, 2 * MIB,
    )
    pillar_parts = exchange(pillar_part, rest)
    out = struct((8, D), F32)
    return call(total_kernel, "total", (out, out), [VMEM, VMEM], (pillar_parts, latent_parts), (), 0, 2 * MIB)


def solution(mesh):
    split = Mesh(mesh.devices.reshape(2, 4, 4, 2, 2), ("grp", "x", "z", "core", "dp"))
    seq = ("x", "z", "core")
    placed = (P("dp", seq, "grp", None, None), P(), P("dp", seq, None, None)) + (P(),) * 10
    out = P(("grp", "x", "z", "core", "dp"), None)
    return jax.shard_map(
        shards, mesh=split, in_specs=placed, out_specs=(out, out), check_vma=False
    )
```

time: 1530 us -> 147 us (0.10)
  waiting for transfers between devices: 1330 us -> 18.2 us
  local copies, waits for them, and re-layouts: 84.2 us -> 4.68 us
  Pallas kernels: 0 us -> 62.7 us
  matrix products: 48.9 us -> 0 us
  blocking collectives: 0 us -> 37.2 us
  other arithmetic: 22.2 us -> 0 us
    reduce_scatter x1 -> x0, waiting for transfers between devices: 648 us -> none  [shards(): lax.psum_scatter(latent_part, ('grp', 'seq', 'dp'), scatter_dimension=0,...]
    unnamed x3 -> x0, waiting for transfers between devices: 644 us -> none
    pallas_call x0 -> x9, Pallas kernels: none -> 62.7 us  [call(): pl.pallas_call(kernel, out_shape=outs, in_specs=in_specs, out_specs=tuple...]
    dot_general x24 -> x0, matrix products: 48.9 us -> none  [the longest x9 24.7 us: project(): return jnp.dot(activations, weight, preferred_element_type=jnp.float32)]
    all_to_all x0 -> x2, blocking collectives: none -> 37.2 us  [exchange(): return lax.all_to_all(values, axes, split_axis=0, concat_axis=0, tiled=True)]
    unnamed x58 -> x18, local copies, waits for them, and re-layouts: 31.5 us -> 3.85 us
    all_to_all x3, waiting for transfers between devices: 36.6 us -> 14.8 us  [exchange(): return lax.all_to_all(values, axes, split_axis=0, concat_axis=0, tiled=True)]
    unnamed x4 -> x0, other arithmetic: 17.3 us -> none
  transfers between devices with their start and end apart: 5 -> 7, of which waited for: 4 -> 4; matrix products, arithmetic and copies ran while one was open for 4% -> 0% of each run, Pallas kernels for 0% -> 19%
where the time goes in v1:
time: 147 us; the launch traced here: 146 us
  Pallas kernels  62.7 us (43%)
  blocking collectives  37.2 us (25%)
  starting transfers between devices  22.2 us (15%)
  waiting for transfers between devices  18.2 us (12%)
  local copies, waits for them, and re-layouts  4.68 us (3%)
    pallas_call x9, Pallas kernels, call(): pl.pallas_call(kernel, out_shape=outs, in_specs=in_specs, out_specs=tuple...  62.7 us
    all_to_all x2, blocking collectives, exchange(): return lax.all_to_all(values, axes, split_axis=0, concat_axis=0, tiled=True)  37.2 us
    all_to_all x3, starting transfers between devices, exchange(): return lax.all_to_all(values, axes, split_axis=0, concat_axis=0, tiled=True)  21.1 us
    all_to_all x3, waiting for transfers between devices, exchange(): return lax.all_to_all(values, axes, split_axis=0, concat_axis=0, tiled=True)  14.8 us
    unnamed x18, local copies, waits for them, and re-layouts  3.85 us
  transfers between devices with their start and end apart: 7, of which 4 were waited for; matrix products, arithmetic and copies ran while one was open for 0% of the time, Pallas kernels for 19%

profile of v1, /device:TPU:0, one launch (start us, length us, event | category | flops | bytes accessed | tf_op | source)
XLA Modules:
  0.0 145.7 jit_solution(5529089708917064177)
XLA Ops:
  0.6 1.2 copy-done
  1.9 0.8 constant_dynamic-slice_fusion
  2.7 6.5 %all-to-all-start.1 = ((bf16[16,16,1024]{2,1,0:T(8,128)(2,1)}), bf16[16,16,1024]{2,1,0:T(8,128)(2,1)S(1)}, u32[]{:S(2)}, u32[]{:S(2)}) async-start(bf16[16,16,1024]{2,1,0:T(8,128)(2,1)} %bitcast.5), calls=%async_computation.1 | async-start | bytes 1048576 | tf_op jit(solution)/shard_map/all_to_all | solution.py:266
  9.2 14.0 %front.1 = (bf16[256,1024]{1,0:T(8,128)(2,1)}, f32[256,1024]{1,0:T(8,128)}, bf16[256,1024]{1,0:T(8,128)(2,1)}, bf16[256,1024]{1,0:T(8,128)(2,1)}, bf16[256,3072]{1,0:T(8,128)(2,1)}, /*index=5*/bf16[256,1024]{1,0:T(8,128)(2,1)}) custom-call(s32[256,1024]{1,0:T(8,128)} %bitcast.26, bf16[1024,1024]{1,0:T(8,128)(2,1)} %pillar_proj.1, f32[1,1024]{1,0:T(1,128)} %bitcast.24, ...), custom_call_target="tpu_custom_call" | custom-call | flops 4294967296 | bytes 20971520 | tf_op jit(solution)/shard_map/front/pallas_call | solution.py:224
  23.3 5.7 %all-to-all-start = ((bf16[16,16,1024]{2,1,0:T(8,128)(2,1)}), bf16[16,16,1024]{2,1,0:T(8,128)(2,1)S(1)}, u32[]{:S(2)}, u32[]{:S(2)}) async-start(bf16[16,16,1024]{2,1,0:T(8,128)(2,1)} %bitcast.20), calls=%async_computation | async-start | bytes 1048576 | tf_op jit(solution)/shard_map/all_to_all | solution.py:266
  29.0 3.3 %mixture.1.dmixed = bf16[256,1024]{1,0:T(8,128)(2,1)} custom-call(bf16[256,1024]{1,0:T(8,128)(2,1)} %bitcast.18, bf16[1024,1024]{1,0:T(8,128)(2,1)} %time_output.1), custom_call_target="tpu_custom_call" | custom-call | flops 536870912 | bytes 3145728 | tf_op jit(solution)/shard_map/mixture/pallas_call | solution.py:224
  32.3 6.5 %all-to-all-done = bf16[16,16,1024]{2,1,0:T(8,128)(2,1)S(1)} async-done(((bf16[16,16,1024]{2,1,0:T(8,128)(2,1)}), bf16[16,16,1024]{2,1,0:T(8,128)(2,1)S(1)}, u32[]{:S(2)}, u32[]{:S(2)}) %all-to-all-start) | async-done | bytes 524320 | tf_op jit(solution)/shard_map/all_to_all | solution.py:266
  38.9 0.8 copy-done.5
  39.7 15.6 %time.1 = bf16[256,1024]{1,0:T(8,128)(2,1)} custom-call(s32[2,4]{1,0:T(2,128)} %valid_frames.1, bf16[256,1024]{1,0:T(8,128)(2,1)} %bitcast.21, bf16[256,1024]{1,0:T(8,128)(2,1)} %bitcast.19, bf16[256,1024]{1,0:T(8,128)(2,1)} %mixture.1.dmixed, f32[1,1024]{1,0:T(1,128)} %bitcast.27, bf16[1024,3072]{1,0:T(8,128)(2,1)} %time_project.1), custom_call_target="tpu_custom_call" | custom-call | flops 4294967296 | bytes 10485760 | tf_op jit(solution)/shard_map/time/pallas_call | solution.py:224
  55.3 14.1 %all_to_all.55 = bf16[16,16,1024]{2,1,0:T(8,128)(2,1)} all-to-all(bf16[16,16,1024]{2,1,0:T(8,128)(2,1)} %bitcast.22), channel_id=1, replica_groups=mesh['grp'=2,'x'=4,'z'=4,'core'=2,'dp'=2] {'z','core','grp'}, dimensions={0} | all-to-all | bytes 1048576 | tf_op jit(solution)/shard_map/all_to_all | solution.py:266
  69.4 14.4 %back.1.dlatent.grad_own = bf16[256,1024]{1,0:T(8,128)(2,1)} custom-call(bf16[256,1024]{1,0:T(8,128)(2,1)} %bitcast.23, bf16[256,3072]{1,0:T(8,128)(2,1)} %get-tuple-element.17.joined, bf16[256,1024]{1,0:T(8,128)(2,1)} %get-tuple-element.18.stream, f32[1,1024]{1,0:T(1,128)} %bitcast.29, bf16[1024,1024]{1,0:T(8,128)(2,1)} %space_output.3, ...), custom_call_target="tpu_custom_call" | custom-call | flops 3758096384 | bytes 14680064 | tf_op jit(solution)/shard_map/back/pallas_call | solution.py:224
  84.0 2.4 %turn.1 = (bf16[512,256]{1,0:T(8,128)(2,1)}, bf16[512,256]{1,0:T(8,128)(2,1)}, bf16[512,256]{1,0:T(8,128)(2,1)}, bf16[512,256]{1,0:T(8,128)(2,1)}) custom-call(bf16[256,1024]{1,0:T(8,128)(2,1)} %get-tuple-element.12.features, bf16[256,1024]{1,0:T(8,128)(2,1)} %get-tuple-element.13.hidden), custom_call_target="tpu_custom_call" | custom-call | bytes 2097152 | tf_op jit(solution)/shard_map/turn/pallas_call | solution.py:224
  86.8 1.4 collective-permute-done.2.other
  88.2 0.7 copy-done.7
  89.1 3.1 %latent_weight.1 = bf16[512,1024]{1,0:T(8,128)(2,1)} custom-call(bf16[512,256]{1,0:T(8,128)(2,1)} %get-tuple-element.20.own, bf16[512,256]{1,0:T(8,128)(2,1)} %copy-done.7, bf16[256,1024]{1,0:T(8,128)(2,1)} %back.1.dlatent.grad_own, bf16[256,1024]{1,0:T(8,128)(2,1)} %copy-done.3), custom_call_target="tpu_custom_call" | custom-call | flops 536870912 | bytes 2097152 | tf_op jit(solution)/shard_map/latent_weight/pallas_call | solution.py:224
  92.2 8.9 %all-to-all-start.4 = ((bf16[64,8,1024]{2,1,0:T(8,128)(2,1)}), bf16[64,8,1024]{2,1,0:T(8,128)(2,1)S(1)}, u32[]{:S(2)}, u32[]{:S(2)}) async-start(bf16[64,8,1024]{2,1,0:T(8,128)(2,1)} %bitcast.15), calls=%async_computation.4 | async-start | bytes 2097152 | tf_op jit(solution)/shard_map/all_to_all | solution.py:266
  101.1 4.4 %token_.1.grad_own = bf16[256,1024]{1,0:T(8,128)(2,1)} custom-call(bf16[256,1024]{1,0:T(8,128)(2,1)} %back.1.dlatent.grad_own, f32[256,1024]{1,0:T(8,128)} %get-tuple-element.19.before, f32[1,1024]{1,0:T(1,128)} %bitcast.25, bf16[1024,1024]{1,0:T(8,128)(2,1)} %latent_proj.3), custom_call_target="tpu_custom_call" | custom-call | flops 536870912 | bytes 4194304 | tf_op jit(solution)/shard_map/token/pallas_call | solution.py:224
  105.6 0.4 collective-permute-start
  106.0 2.0 %collective-permute-done.other = bf16[512,256]{1,0:T(8,128)(2,1)S(1)} collective-permute-done((bf16[512,256]{1,0:T(8,128)(2,1)S(1)}, bf16[512,256]{1,0:T(8,128)(2,1)S(1)}, u32[]{:S(2)}, u32[]{:S(2)}) %collective-permute-start) | collective-permute-done | bytes 262176 | tf_op jit(solution)/shard_map/ppermute | solution.py:298
  108.0 0.7 copy-done.6
  108.9 3.1 %pillar_weight.1 = bf16[512,1024]{1,0:T(8,128)(2,1)} custom-call(bf16[512,256]{1,0:T(8,128)(2,1)} %get-tuple-element.14.own, bf16[512,256]{1,0:T(8,128)(2,1)} %copy-done.6, bf16[256,1024]{1,0:T(8,128)(2,1)} %token_.1.grad_own, bf16[256,1024]{1,0:T(8,128)(2,1)} %copy-done.4), custom_call_target="tpu_custom_call" | custom-call | flops 536870912 | bytes 2097152 | tf_op jit(solution)/shard_map/pillar_weight/pallas_call | solution.py:224
  111.9 8.2 %all-to-all-done.4 = bf16[64,8,1024]{2,1,0:T(8,128)(2,1)S(1)} async-done(((bf16[64,8,1024]{2,1,0:T(8,128)(2,1)}), bf16[64,8,1024]{2,1,0:T(8,128)(2,1)S(1)}, u32[]{:S(2)}, u32[]{:S(2)}) %all-to-all-start.4) | async-done | bytes 1048608 | tf_op jit(solution)/shard_map/all_to_all | solution.py:266
  120.2 23.1 %all_to_all.56 = bf16[64,8,1024]{2,1,0:T(8,128)(2,1)} all-to-all(bf16[64,8,1024]{2,1,0:T(8,128)(2,1)} %bitcast.16), channel_id=1, replica_groups=mesh['grp'=2,'x'=4,'z'=4,'core'=2,'dp'=2] {'grp','x','z','dp'}, dimensions={0} | all-to-all | bytes 2097152 | tf_op jit(solution)/shard_map/all_to_all | solution.py:266
  143.3 2.5 %total.1 = (f32[8,1024]{1,0:T(8,128)}, f32[8,1024]{1,0:T(8,128)}) custom-call(bf16[512,1024]{1,0:T(8,128)(2,1)} %bitcast.17, bf16[512,1024]{1,0:T(8,128)(2,1)} %bitcast.14), custom_call_target="tpu_custom_call" | custom-call | bytes 2097152 | tf_op jit(solution)/shard_map/total/pallas_call | solution.py:224
  (20 shorter events, 1.1 us)
Async XLA Ops:
  0.6 1.2 copy-start
  2.7 20.6 %all-to-all-start.1 = ((bf16[16,16,1024]{2,1,0:T(8,128)(2,1)}), bf16[16,16,1024]{2,1,0:T(8,128)(2,1)S(1)}, u32[]{:S(2)}, u32[]{:S(2)}) async-start(bf16[16,16,1024]{2,1,0:T(8,128)(2,1)} %bitcast.5), calls=%async_computation.1 | async-start | bytes 1048576 | tf_op jit(solution)/shard_map/all_to_all | solution.py:266
  23.3 5.7 %copy-start.2 = (bf16[16,16,1024]{2,1,0:T(8,128)(2,1)}, bf16[16,16,1024]{2,1,0:T(8,128)(2,1)S(1)}, u32[]{:S(2)}) copy-start(bf16[16,16,1024]{2,1,0:T(8,128)(2,1)S(1)} %all-to-all-done.1) | copy-start | bytes 1572868
  23.3 15.6 %all-to-all-start = ((bf16[16,16,1024]{2,1,0:T(8,128)(2,1)}), bf16[16,16,1024]{2,1,0:T(8,128)(2,1)S(1)}, u32[]{:S(2)}, u32[]{:S(2)}) async-start(bf16[16,16,1024]{2,1,0:T(8,128)(2,1)} %bitcast.20), calls=%async_computation | async-start | bytes 1048576 | tf_op jit(solution)/shard_map/all_to_all | solution.py:266
  38.9 0.8 copy-start.5
  83.7 4.5 %collective-permute-start.3 = (bf16[256,1024]{1,0:T(8,128)(2,1)}, bf16[256,1024]{1,0:T(8,128)(2,1)S(1)}, u32[]{:S(2)}, u32[]{:S(2)}) collective-permute-start(bf16[256,1024]{1,0:T(8,128)(2,1)} %back.1.dlatent.grad_own), channel_id=1, source_target_pairs={{0,2},{2,0},{1,3},{3,1},{4,6},{6,4},{5,7},{7,5},{8,10},{10,8},{9,1... | collective-permute-start | bytes 1572872 | tf_op jit(solution)/shard_map/ppermute | solution.py:324
  86.4 1.7 %collective-permute-start.2 = (bf16[512,256]{1,0:T(8,128)(2,1)}, bf16[512,256]{1,0:T(8,128)(2,1)S(1)}, u32[]{:S(2)}, u32[]{:S(2)}) collective-permute-start(bf16[512,256]{1,0:T(8,128)(2,1)} %get-tuple-element.21), channel_id=1, source_target_pairs={{0,2},{2,0},{1,3},{3,1},{4,6},{6,4},{5,7},{7,5},{8,10},{10,8},{9,1... | collective-permute-start | bytes 786440 | tf_op jit(solution)/shard_map/ppermute | solution.py:299
  88.2 0.7 copy-start.7
  88.2 0.9 copy-start.3
  92.2 28.0 %all-to-all-start.4 = ((bf16[64,8,1024]{2,1,0:T(8,128)(2,1)}), bf16[64,8,1024]{2,1,0:T(8,128)(2,1)S(1)}, u32[]{:S(2)}, u32[]{:S(2)}) async-start(bf16[64,8,1024]{2,1,0:T(8,128)(2,1)} %bitcast.15), calls=%async_computation.4 | async-start | bytes 2097152 | tf_op jit(solution)/shard_map/all_to_all | solution.py:266
  101.1 4.5 %copy-start.8 = (bf16[512,256]{1,0:T(8,128)(2,1)S(1)}, bf16[512,256]{1,0:T(8,128)(2,1)}, u32[]{:S(2)}) copy-start(bf16[512,256]{1,0:T(8,128)(2,1)} %get-tuple-element.15) | copy-start | bytes 786436
  105.5 2.5 %collective-permute-start.1 = (bf16[256,1024]{1,0:T(8,128)(2,1)}, bf16[256,1024]{1,0:T(8,128)(2,1)S(1)}, u32[]{:S(2)}, u32[]{:S(2)}) collective-permute-start(bf16[256,1024]{1,0:T(8,128)(2,1)} %token_.1.grad_own), channel_id=1, source_target_pairs={{0,2},{2,0},{1,3},{3,1},{4,6},{6,4},{5,7},{7,5},{8,10},{10,8},{9,1... | collective-permute-start | bytes 1572872 | tf_op jit(solution)/shard_map/ppermute | solution.py:335
  105.6 2.4 %collective-permute-start = (bf16[512,256]{1,0:T(8,128)(2,1)S(1)}, bf16[512,256]{1,0:T(8,128)(2,1)S(1)}, u32[]{:S(2)}, u32[]{:S(2)}) collective-permute-start(bf16[512,256]{1,0:T(8,128)(2,1)S(1)} %copy-done.8), channel_id=1, source_target_pairs={{0,2},{2,0},{1,3},{3,1},{4,6},{6,4},{5,7},{7,5},{8,10},{10,8},{9,1... | collective-permute-start | bytes 786440 | tf_op jit(solution)/shard_map/ppermute | solution.py:298
  108.0 0.7 copy-start.6
  108.0 0.9 copy-start.4
  120.2 23.1 %copy-start.1 = (bf16[64,8,1024]{2,1,0:T(8,128)(2,1)}, bf16[64,8,1024]{2,1,0:T(8,128)(2,1)S(1)}, u32[]{:S(2)}) copy-start(bf16[64,8,1024]{2,1,0:T(8,128)(2,1)S(1)} %all-to-all-done.4) | copy-start | bytes 3145732

commit v2 on v1

--- a/solution.py
+++ b/solution.py
@@ -16,7 +16,7 @@
 SCALE = HEAD**-0.5
 VMEM = pl.BlockSpec(memory_space=pltpu.VMEM)
 SMEM = pl.BlockSpec(memory_space=pltpu.SMEM)
-ANY = pl.BlockSpec(memory_space=pl.ANY)
+HBM = pl.BlockSpec(memory_space=pltpu.HBM)
 
 
 def dot(a, b):
@@ -86,49 +86,74 @@
 
 
 def front_kernel(
-    counts, pillar_proj, pillar_gain, latent_proj, input_proj, space_gain, space_project,
-    space_output, features, before, hidden, stream, joined, spaced,
-    w_pillar, w_latent, w_input, w_project, w_output, mixed, sems,
+    counts, cotangent, pillar_proj, pillar_gain, latent_proj, input_proj, space_gain,
+    space_project, space_output, features, before, hidden, stream, joined, packed,
+    w_pillar, w_latent, w_input, w_project, w_output, counted, mixed,
+    v_features, v_before, v_hidden, v_stream, v_joined, sems, out_sems,
 ):
     copies = fetch(
         [
+            (counts, counted),
             (pillar_proj, w_pillar),
             (latent_proj, w_latent),
             (input_proj, w_input),
             (space_project, w_project),
             (space_output, w_output),
+            (cotangent.at[lax.axis_index("grp")], packed.at[:, 1]),
         ],
         sems,
     )
-    x = jnp.log(counts[...].astype(F32) + 1.0).astype(BF16)
-    features[...] = x
+    saves = [
+        pltpu.make_async_copy(src, dst, out_sems.at[k])
+        for k, (src, dst) in enumerate(
+            (
+                (v_features, features),
+                (v_before, before),
+                (v_hidden, hidden),
+                (v_stream, stream),
+                (v_joined, joined),
+            )
+        )
+    ]
     copies[0].wait()
+    x = jnp.log(counted[...].astype(F32) + 1.0).astype(BF16)
+    v_features[...] = x
+    saves[0].start()
+    copies[1].wait()
     b = dot(x, w_pillar[...])
-    before[...] = b
+    v_before[...] = b
+    saves[1].start()
     n = b * inverse_rms(b) * pillar_gain[...]
     hid = (0.5 * n * (1.0 + jnp.tanh(GELU_A * (n + GELU_B * n * n * n)))).astype(BF16)
-    hidden[...] = hid
-    copies[1].wait()
+    v_hidden[...] = hid
+    saves[2].start()
+    copies[2].wait()
     lat = dot(hid, w_latent[...]).astype(BF16)
-    copies[2].wait()
+    copies[3].wait()
     s = dot(lat, w_input[...]).astype(BF16)
-    stream[...] = s
+    v_stream[...] = s
+    saves[3].start()
     s = s.astype(F32)
     u = (s * inverse_rms(s) * space_gain[...]).astype(BF16)
-    copies[3].wait()
+    copies[4].wait()
     for part in range(3):
         cols = slice(part * D, (part + 1) * D)
-        joined[:, cols] = dot(u, w_project[:, cols]).astype(BF16)
+        v_joined[:, cols] = dot(u, w_project[:, cols]).astype(BF16)
+    saves[4].start()
 
     def head(h, carry):
-        q, k, v, iq, ik, qn, kn = head_parts(joined, h)
+        q, k, v, iq, ik, qn, kn = head_parts(v_joined, h)
         weights = softmax(qn, kn, None).astype(BF16)
         mixed[:, pl.ds(pl.multiple_of(h * HEAD, HEAD), HEAD)] = dot(weights, v).astype(BF16)
         return carry
 
-    lax.fori_loop(0, HEADS, head, 0)
-    copies[4].wait()
-    spaced[...] = (stream[...].astype(F32) + dot(mixed[...], w_output[...])).astype(BF16)
+    lax.fori_loop(0, HEADS, head, 0, unroll=True)
+    copies[5].wait()
+    spaced = (v_stream[...].astype(F32) + dot(mixed[...], w_output[...])).astype(BF16)
+    packed[:, 0] = spaced.reshape(16, 16, D)
+    copies[6].wait()
+    for save in saves:
+        save.wait()
 
 
 def turn_kernel(features, hidden, feat_own, feat_send, hid_own, hid_send, turned):
@@ -139,25 +164,20 @@
         send[...] = turned[:, 1 - core].reshape(512, TOK)
 
 
-def mixture_kernel(cot, time_output, out):
-    out[...] = dot_nt(cot[...], time_output[...]).astype(BF16)
-
-
 def time_kernel(
-    valid_frames, spaced, cot, dmixed, time_gain, time_project, grad,
-    w_project, joined, djoined, masked, sems,
+    valid_frames, packed, time_gain, w_project, w_output, grad, joined, dmixed, djoined, masked
 ):
-    copies = fetch([(time_project, w_project)], sems)
     valid = valid_frames[lax.axis_index("dp"), lax.axis_index("x")]
     row = lax.broadcasted_iota(jnp.int32, (TOK, TOK), 0)
     col = lax.broadcasted_iota(jnp.int32, (TOK, TOK), 1)
     e = col // FRAMES
     seen = (row % FRAMES == col % FRAMES) & (e <= row // FRAMES) & (e < valid)
     masked[...] = seen.astype(F32)
-    s = spaced[...].astype(F32)
+    cot = packed[:, 1].reshape(TOK, D)
+    dmixed[...] = dot_nt(cot, w_output[...]).astype(BF16)
+    s = packed[:, 0].reshape(TOK, D).astype(F32)
     inverse = inverse_rms(s)
     u = (s * inverse * time_gain[...]).astype(BF16)
-    copies[0].wait()
     for part in range(3):
         cols = slice(part * D, (part + 1) * D)
         joined[:, cols] = dot(u, w_project[:, cols]).astype(BF16)
@@ -166,32 +186,26 @@
         attention_back(joined, dmixed, djoined, masked[...], h)
         return carry
 
-    lax.fori_loop(0, HEADS, head, 0)
+    lax.fori_loop(0, HEADS, head, 0, unroll=True)
     du = dot_nt(djoined[...], w_project[...]).astype(BF16).astype(F32) * time_gain[...]
-    s = spaced[...].astype(F32)
-    grad[...] = (cot[...].astype(F32) + norm_back(s, inverse_rms(s), du)).astype(BF16)
+    s = packed[:, 0].reshape(TOK, D).astype(F32)
+    cot = packed[:, 1].reshape(TOK, D).astype(F32)
+    grad[...] = (cot + norm_back(s, inverse_rms(s), du)).astype(BF16)
 
 
 def back_kernel(
-    dspaced, joined, stream, space_gain, space_output, space_project, input_proj, dlatent,
-    w_output, w_project, w_input, dmixed, djoined, sems,
+    dspaced, joined, stream, space_gain, w_output, w_project, w_input, dlatent, dmixed, djoined
 ):
-    copies = fetch(
-        [(space_output, w_output), (space_project, w_project), (input_proj, w_input)], sems
-    )
-    copies[0].wait()
     dmixed[...] = dot_nt(dspaced[...], w_output[...]).astype(BF16)
 
     def head(h, carry):
         attention_back(joined, dmixed, djoined, None, h)
         return carry
 
-    lax.fori_loop(0, HEADS, head, 0)
-    copies[1].wait()
+    lax.fori_loop(0, HEADS, head, 0, unroll=True)
     du = dot_nt(djoined[...], w_project[...]).astype(BF16).astype(F32) * space_gain[...]
     s = stream[...].astype(F32)
     dstream = (dspaced[...].astype(F32) + norm_back(s, inverse_rms(s), du)).astype(BF16)
-    copies[2].wait()
     dlatent[...] = dot_nt(dstream, w_input[...]).astype(BF16)
 
 
@@ -206,26 +220,32 @@
     dbefore[...] = norm_back(b, inverse, dn).astype(BF16)
 
 
-def weight_kernel(own, other, grad_own, grad_other, out):
+def latent_kernel(own, other, grad_own, grad_other, out):
     out[...] = (dot(own[...], grad_own[...]) + dot(other[...], grad_other[...])).astype(BF16)
 
 
-def total_kernel(a, b, out_a, out_b):
-    for src, out in ((a, out_a), (b, out_b)):
-        out[...] = jnp.sum(src[...].astype(F32).reshape(64, 8, D), axis=0)
+def pillar_kernel(own, other, grad_own, grad_other, latent, out):
+    part = dot(own[...], grad_own[...]) + dot(other[...], grad_other[...])
+    out[:, 0] = part.reshape(64, 8, D).astype(BF16)
+    out[:, 1] = latent[...].reshape(64, 8, D)
+
+
+def total_kernel(parts, pillar, latent):
+    for k, out in ((0, pillar), (1, latent)):
+        out[...] = jnp.sum(parts[:, k].astype(F32), axis=0)
 
 
 def struct(shape, dtype):
     return jax.ShapeDtypeStruct(shape, dtype)
 
 
-def call(kernel, name, outs, in_specs, args, scratch=(), flops=0, bytes_accessed=0, limit=None):
+def call(kernel, name, outs, in_specs, args, scratch=(), flops=0, bytes_accessed=0, limit=28 << 20, out_specs=None):
     many = isinstance(outs, tuple)
     return pl.pallas_call(
         kernel,
         out_shape=outs,
         in_specs=in_specs,
-        out_specs=tuple(VMEM for _ in outs) if many else VMEM,
+        out_specs=out_specs or (tuple(VMEM for _ in outs) if many else VMEM),
         scratch_shapes=list(scratch),
         name=name,
         cost_estimate=pl.CostEstimate(
@@ -256,7 +276,6 @@
 ):
     rows = struct((TOK, D), BF16)
     scene = ("z", "core", "grp")
-    rest = ("grp", "x", "z", "dp")
     swap = ((0, 1), (1, 0))
     pillar_gain = pillar_gain.reshape(1, D)
     space_gain = space_gain.reshape(1, D)
@@ -265,26 +284,28 @@
     def exchange(values, axes):
         return lax.all_to_all(values, axes, split_axis=0, concat_axis=0, tiled=True)
 
-    own_cot = lax.dynamic_index_in_dim(cotangent[0], lax.axis_index("grp"), 0, keepdims=False)
-    cot = exchange(own_cot, scene)
-
-    wide = lambda n: pltpu.VMEM((D, n * D), BF16)
-    features, before, hidden, stream, joined, spaced = call(
+    wide = lambda n, dtype=BF16: pltpu.VMEM((D, n * D), dtype)
+    tall = lambda n, dtype=BF16: pltpu.VMEM((TOK, n * D), dtype)
+    features, before, hidden, stream, joined, packed = call(
         front_kernel,
         "front",
-        (rows, struct((TOK, D), F32), rows, rows, struct((TOK, 3 * D), BF16), rows),
-        [VMEM, ANY, VMEM, ANY, ANY, VMEM, ANY, ANY],
+        (rows, struct((TOK, D), F32), rows, rows, struct((TOK, 3 * D), BF16),
+         struct((16, 2, 16, D), BF16)),
+        [HBM, HBM, HBM, VMEM, HBM, HBM, VMEM, HBM, HBM],
         (
-            counts.reshape(TOK, D), pillar_proj, pillar_gain, latent_proj, input_proj,
-            space_gain, space_project, space_output,
+            counts.reshape(TOK, D), cotangent.reshape(2, 16, 16, D), pillar_proj, pillar_gain,
+            latent_proj, input_proj, space_gain, space_project, space_output,
         ),
-        [wide(1), wide(1), wide(1), wide(3), wide(1), pltpu.VMEM((TOK, D), BF16),
-         pltpu.SemaphoreType.DMA((5,))],
+        [wide(1), wide(1), wide(1), wide(3), wide(1), tall(1, jnp.int32), tall(1),
+         tall(1), tall(1, F32), tall(1), tall(1), tall(3),
+         pltpu.SemaphoreType.DMA((7,)), pltpu.SemaphoreType.DMA((5,))],
         8 * UNIT,
         20 * MIB,
-    )
+        None,
+        [HBM, HBM, HBM, HBM, HBM, VMEM],
+    )
+    packed = exchange(packed, scene)
     half = struct((512, TOK), BF16)
-    spaced_tok = exchange(spaced, scene)
     feat_own, feat_send, hid_own, hid_send = call(
         turn_kernel,
         "turn",
@@ -297,16 +318,14 @@
     )
     feat_other = lax.ppermute(feat_send, "core", swap)
     hid_other = lax.ppermute(hid_send, "core", swap)
-    dmixed = call(mixture_kernel, "mixture", rows, [VMEM, VMEM], (cot, time_output), (), UNIT, 3 * MIB)
     grad_tok = call(
         time_kernel,
         "time",
         rows,
-        [SMEM, VMEM, VMEM, VMEM, VMEM, ANY],
-        (valid_frames, spaced_tok, cot, dmixed, time_gain, time_project),
-        [wide(3), pltpu.VMEM((TOK, 3 * D), BF16), pltpu.VMEM((TOK, 3 * D), BF16),
-         pltpu.VMEM((TOK, TOK), F32), pltpu.SemaphoreType.DMA((1,))],
-        8 * UNIT,
+        [SMEM, VMEM, VMEM, VMEM, VMEM],
+        (valid_frames, packed, time_gain, time_project, time_output),
+        [tall(3), tall(1), tall(3), pltpu.VMEM((TOK, TOK), F32)],
+        9 * UNIT,
         10 * MIB,
     )
     dspaced = exchange(grad_tok, scene)
@@ -314,10 +333,9 @@
         back_kernel,
         "back",
         rows,
-        [VMEM, VMEM, VMEM, VMEM, ANY, ANY, ANY],
+        [VMEM] * 7,
         (dspaced, joined, stream, space_gain, space_output, space_project, input_proj),
-        [wide(1), wide(3), wide(1), pltpu.VMEM((TOK, D), BF16), pltpu.VMEM((TOK, 3 * D), BF16),
-         pltpu.SemaphoreType.DMA((3,))],
+        [tall(1), tall(3)],
         7 * UNIT,
         14 * MIB,
     )
@@ -333,19 +351,17 @@
         4 * MIB,
     )
     dbefore_other = lax.ppermute(dbefore, "core", swap)
-    partial = struct((512, D), BF16)
     latent_part = call(
-        weight_kernel, "latent_weight", partial, [VMEM] * 4,
+        latent_kernel, "latent_weight", struct((512, D), BF16), [VMEM] * 4,
         (hid_own, hid_other, dlatent, dlatent_other), (), UNIT, 2 * MIB,
     )
-    latent_parts = exchange(latent_part, rest)
-    pillar_part = call(
-        weight_kernel, "pillar_weight", partial, [VMEM] * 4,
-        (feat_own, feat_other, dbefore, dbefore_other), (), UNIT, 2 * MIB,
-    )
-    pillar_parts = exchange(pillar_part, rest)
+    parts = call(
+        pillar_kernel, "pillar_weight", struct((64, 2, 8, D), BF16), [VMEM] * 5,
+        (feat_own, feat_other, dbefore, dbefore_other, latent_part), (), UNIT, 4 * MIB,
+    )
+    parts = exchange(parts, ("grp", "x", "z", "dp"))
     out = struct((8, D), F32)
-    return call(total_kernel, "total", (out, out), [VMEM, VMEM], (pillar_parts, latent_parts), (), 0, 2 * MIB)
+    return call(total_kernel, "total", (out, out), [VMEM], (parts,), (), 0, 2 * MIB)
 
 
 def solution(mesh):

time: 147 us -> 113 us (0.77)
  blocking collectives: 37.2 us -> 74.2 us
  Pallas kernels: 62.7 us -> 32.1 us
  starting transfers between devices: 22.2 us -> 1.26 us
  waiting for transfers between devices: 18.2 us -> 1.03 us
  local copies, waits for them, and re-layouts: 4.68 us -> 2.86 us
    all_to_all x2 -> x3, blocking collectives: 37.2 us -> 74.2 us  [exchange(): return lax.all_to_all(values, axes, split_axis=0, concat_axis=0, tiled=True)]
    pallas_call x9 -> x8, Pallas kernels: 62.7 us -> 32.1 us  [call(): pl.pallas_call(kernel, out_shape=outs, in_specs=in_specs, out_specs=out_s...]
    all_to_all x3 -> x0, starting transfers between devices: 21.1 us -> none  [exchange(): return lax.all_to_all(values, axes, split_axis=0, concat_axis=0, tiled=True)]
    all_to_all x3 -> x0, waiting for transfers between devices: 14.8 us -> none  [exchange(): return lax.all_to_all(values, axes, split_axis=0, concat_axis=0, tiled=True)]
    ppermute x1, waiting for transfers between devices: 1.98 us -> 0.01 us  [shards(): feat_other = lax.ppermute(feat_send, 'core', swap)]
    unnamed x18 -> x32, local copies, waits for them, and re-layouts: 3.85 us -> 2.86 us
  transfers between devices with their start and end apart: 7 -> 4, of which waited for: 4 -> 1; matrix products, arithmetic and copies ran while one was open for 0% -> 0% of each run, Pallas kernels for 19% -> 2%
where the time goes in v2:
time: 113 us; the launch traced here: 112 us
  blocking collectives  74.2 us (66%)
  Pallas kernels  32.1 us (28%)
  local copies, waits for them, and re-layouts  2.86 us (3%)
  starting transfers between devices  1.26 us (1%)
    all_to_all x3, blocking collectives, exchange(): return lax.all_to_all(values, axes, split_axis=0, concat_axis=0, tiled=True)  74.2 us
    pallas_call x8, Pallas kernels, call(): pl.pallas_call(kernel, out_shape=outs, in_specs=in_specs, out_specs=out_s...  32.1 us
    unnamed x32, local copies, waits for them, and re-layouts  2.86 us
  transfers between devices with their start and end apart: 4, of which 1 were waited for; matrix products, arithmetic and copies ran while one was open for 0% of the time, Pallas kernels for 2%

profile of v2, /device:TPU:0, one launch (start us, length us, event | category | flops | bytes accessed | tf_op | source)
XLA Modules:
  0.0 112.3 jit_solution(10061115929654761065)
XLA Ops:
  0.7 11.3 %front.1 = (bf16[256,1024]{1,0:T(8,128)(2,1)}, f32[256,1024]{1,0:T(8,128)}, bf16[256,1024]{1,0:T(8,128)(2,1)}, bf16[256,1024]{1,0:T(8,128)(2,1)}, bf16[256,3072]...) custom-call(s32[256,1024]{1,0:T(8,128)} %bitcast.16, bf16[2,16,16,1024]{3,2,1,0:T(8,128)(2,1)} %bitcast.17, ...), custom_call_target="tpu_custom_call" | custom-call | flops 4294967296 | bytes 20971520 | tf_op jit(solution)/shard_map/front/pallas_call | solution.py:244
  12.0 0.0 copy-start.13
  12.0 0.0 slice-start
  12.0 22.3 %all_to_all.21.packed = bf16[16,2,16,1024]{3,2,1,0:T(8,128)(2,1)S(1)} all-to-all(bf16[16,2,16,1024]{3,2,1,0:T(8,128)(2,1)} %get-tuple-element.16), channel_id=1, replica_groups=mesh['grp'=2,'x'=4,'z'=4,'core'=2,'dp'=2] {'z','core','grp'}, dimensions={0} | all-to-all | bytes 2097152 | tf_op jit(solution)/shard_map/all_to_all | solution.py:285
  34.3 0.0 copy-start.8
  34.3 2.8 %copy-done.8 = bf16[1024,3072]{1,0:T(8,128)(2,1)S(1)} copy-done((bf16[1024,3072]{1,0:T(8,128)(2,1)S(1)}, bf16[1024,3072]{1,0:T(8,128)(2,1)}, u32[]{:S(2)}) %copy-start.8) | copy-done | bytes 6291480
  37.2 9.1 %time.1 = bf16[256,1024]{1,0:T(8,128)(2,1)S(1)} custom-call(s32[2,4]{1,0:T(2,128)S(1)} %copy-done.13, bf16[16,2,16,1024]{3,2,1,0:T(8,128)(2,1)S(1)} %all_to_all.21.packed, f32[1,1024]{1,0:T(1,128)S(1)} %bitcast.15, bf16[1024,3072]{1,0:T(8,128)(2,1)S(1)} %copy-done.8, bf16[1024,1024]{1,0:T(8,128)(2,1)S(1)} %copy-done.9), custom_call_target="tpu_custom_call" | custom-call | flops 4831838208 | bytes 10485760 | tf_op jit(solution)/shard_map/time/pallas_call | solution.py:244
  46.3 13.2 %all_to_all.22 = bf16[16,16,1024]{2,1,0:T(8,128)(2,1)S(1)} all-to-all(bf16[16,16,1024]{2,1,0:T(8,128)(2,1)S(1)} %bitcast.10), channel_id=1, replica_groups=mesh['grp'=2,'x'=4,'z'=4,'core'=2,'dp'=2] {'z','core','grp'}, dimensions={0} | all-to-all | bytes 1048576 | tf_op jit(solution)/shard_map/all_to_all | solution.py:285
  59.5 0.0 copy-start
  59.5 0.0 copy-start.6
  59.6 7.3 %back.1.dlatent.grad_own = bf16[256,1024]{1,0:T(8,128)(2,1)S(1)} custom-call(bf16[256,1024]{1,0:T(8,128)(2,1)S(1)} %bitcast.9, bf16[256,3072]{1,0:T(8,128)(2,1)S(1)} %copy-done.10, bf16[256,1024]{1,0:T(8,128)(2,1)S(1)} %copy-done.11, f32[1,1024]{1,0:T(1,128)S(1)} %bitcast.14, bf16[1024,1024]{1,0:T(8,128)(2,1)S(1)} %copy-done.2, ...), custom_call_target="tpu_custom_call" | custom-call | flops 3758096384 | bytes 14680064 | tf_op jit(solution)/shard_map/back/pallas_call | solution.py:244
  66.9 0.3 collective-permute-start.3
  67.2 1.5 %token_.1.grad_own = bf16[256,1024]{1,0:T(8,128)(2,1)S(1)} custom-call(bf16[256,1024]{1,0:T(8,128)(2,1)S(1)} %back.1.dlatent.grad_own, f32[256,1024]{1,0:T(8,128)S(1)} %copy-done.3, f32[1,1024]{1,0:T(1,128)S(1)} %bitcast.12, bf16[1024,1024]{1,0:T(8,128)(2,1)S(1)} %copy-done), custom_call_target="tpu_custom_call" | custom-call | flops 536870912 | bytes 4194304 | tf_op jit(solution)/shard_map/token/pallas_call | solution.py:244
  68.7 0.4 collective-permute-start.1
  69.1 0.4 turn.1
  69.6 0.3 collective-permute-start.2
  69.8 0.3 collective-permute-start
  70.1 1.0 collective-permute-done.2.other
  71.2 0.0 collective-permute-done.3.grad_other
  71.2 0.7 latent_weight.1.latent
  71.9 0.0 collective-permute-done.other
  71.9 0.7 pillar_weight.1
  72.6 38.7 %all_to_all.23.parts = bf16[64,2,8,1024]{3,2,1,0:T(8,128)(2,1)S(1)} all-to-all(bf16[64,2,8,1024]{3,2,1,0:T(8,128)(2,1)S(1)} %pillar_weight.1), channel_id=1, replica_groups=mesh['grp'=2,'x'=4,'z'=4,'core'=2,'dp'=2] {'grp','x','z','dp'}, dimensions={0} | all-to-all | bytes 4194304 | tf_op jit(solution)/shard_map/all_to_all | solution.py:285
  111.3 0.9 total.1
  (28 shorter events, 0.1 us)
Async XLA Ops:
  0.6 33.7 %copy-start.9 = (bf16[1024,1024]{1,0:T(8,128)(2,1)S(1)}, bf16[1024,1024]{1,0:T(8,128)(2,1)}, u32[]{:S(2)}) copy-start(bf16[1024,1024]{1,0:T(8,128)(2,1)} %w_output.2) | copy-start | bytes 6291460
  0.6 33.7 %copy-start.12 = (f32[1024]{0:T(1024)S(1)}, f32[1024]{0:T(1024)}, u32[]{:S(2)}) copy-start(f32[1024]{0:T(1024)} %param.23) | copy-start | bytes 12292
  12.0 22.3 %copy-start.13 = (s32[2,4]{1,0:T(2,128)S(1)}, s32[2,4]{1,0:T(2,128)}, u32[]{:S(2)}) copy-start(s32[2,4]{1,0:T(2,128)} %valid_frames.1) | copy-start | bytes 100
  12.0 47.5 %slice-start = ((s8[6291456]{0:T(1024)(128)(4,1)}), s8[4194304]{0:T(1024)(128)(4,1)S(1)}, s32[]{:S(2)}) async-start(s8[6291456]{0:T(1024)(128)(4,1)} %bitcast.7), calls=%async_computation.3 | async-start | bytes 8388608
  34.3 2.8 %copy-start.8 = (bf16[1024,3072]{1,0:T(8,128)(2,1)S(1)}, bf16[1024,3072]{1,0:T(8,128)(2,1)}, u32[]{:S(2)}) copy-start(bf16[1024,3072]{1,0:T(8,128)(2,1)} %w_project.2) | copy-start | bytes 18874372
  37.1 22.3 %slice-start.1 = ((s8[6291456]{0:T(1024)(128)(4,1)}), s8[2097152]{0:T(1024)(128)(4,1)S(1)}, s32[]{:S(2)}) async-start(s8[6291456]{0:T(1024)(128)(4,1)} %bitcast.7), calls=%async_computation.4 | async-start | bytes 4194304
  37.1 22.3 %copy-start.1 = (bf16[1024,1024]{1,0:T(8,128)(2,1)S(1)}, bf16[1024,1024]{1,0:T(8,128)(2,1)}, u32[]{:S(2)}) copy-start(bf16[1024,1024]{1,0:T(8,128)(2,1)} %w_input.1) | copy-start | bytes 6291460
  37.1 22.3 %copy-start.2 = (bf16[1024,1024]{1,0:T(8,128)(2,1)S(1)}, bf16[1024,1024]{1,0:T(8,128)(2,1)}, u32[]{:S(2)}) copy-start(bf16[1024,1024]{1,0:T(8,128)(2,1)} %w_output.3) | copy-start | bytes 6291460
  37.1 22.3 %copy-start.7 = (f32[1024]{0:T(1024)S(1)}, f32[1024]{0:T(1024)}, u32[]{:S(2)}) copy-start(f32[1024]{0:T(1024)} %param.20) | copy-start | bytes 12292
  37.1 22.4 %copy-start.10 = (bf16[256,3072]{1,0:T(8,128)(2,1)S(1)}, bf16[256,3072]{1,0:T(8,128)(2,1)}, u32[]{:S(2)}) copy-start(bf16[256,3072]{1,0:T(8,128)(2,1)} %get-tuple-element.17.joined) | copy-start | bytes 4718596
  37.1 22.4 %copy-start.11 = (bf16[256,1024]{1,0:T(8,128)(2,1)S(1)}, bf16[256,1024]{1,0:T(8,128)(2,1)}, u32[]{:S(2)}) copy-start(bf16[256,1024]{1,0:T(8,128)(2,1)} %get-tuple-element.18.stream) | copy-start | bytes 1572868
  59.5 7.6 %copy-start = (bf16[1024,1024]{1,0:T(8,128)(2,1)S(1)}, bf16[1024,1024]{1,0:T(8,128)(2,1)}, u32[]{:S(2)}) copy-start(bf16[1024,1024]{1,0:T(8,128)(2,1)} %latent_proj.3) | copy-start | bytes 6291460
  59.5 7.6 %copy-start.3 = (f32[256,1024]{1,0:T(8,128)S(1)}, f32[256,1024]{1,0:T(8,128)}, u32[]{:S(2)}) copy-start(f32[256,1024]{1,0:T(8,128)} %get-tuple-element.19.before) | copy-start | bytes 3145732
  59.5 7.6 %copy-start.6 = (f32[1024]{0:T(1024)S(1)}, f32[1024]{0:T(1024)}, u32[]{:S(2)}) copy-start(f32[1024]{0:T(1024)} %param.17) | copy-start | bytes 12292
  66.9 4.3 %collective-permute-start.3 = (bf16[256,1024]{1,0:T(8,128)(2,1)S(1)}, bf16[256,1024]{1,0:T(8,128)(2,1)S(1)}, u32[]{:S(2)}, u32[]{:S(2)}) collective-permute-start(bf16[256,1024]{1,0:T(8,128)(2,1)S(1)} %back.1.dlatent.grad_own), channel_id=1, source_target_pairs={{0,2},{2,0},{1,3},{3,1},{4,6},{6,4},{5,7},{7,5},{8,10},{10,8},{9,1... | collective-permute-start | bytes 1572872 | tf_op jit(solution)/shard_map/ppermute | solution.py:342
  67.2 2.0 %copy-start.4 = (bf16[256,1024]{1,0:T(8,128)(2,1)S(1)}, bf16[256,1024]{1,0:T(8,128)(2,1)}, u32[]{:S(2)}) copy-start(bf16[256,1024]{1,0:T(8,128)(2,1)} %get-tuple-element.12.features) | copy-start | bytes 1572868
  67.2 2.0 %copy-start.5 = (bf16[256,1024]{1,0:T(8,128)(2,1)S(1)}, bf16[256,1024]{1,0:T(8,128)(2,1)}, u32[]{:S(2)}) copy-start(bf16[256,1024]{1,0:T(8,128)(2,1)} %get-tuple-element.13.hidden) | copy-start | bytes 1572868
  68.7 3.2 %collective-permute-start.1 = (bf16[256,1024]{1,0:T(8,128)(2,1)S(1)}, bf16[256,1024]{1,0:T(8,128)(2,1)S(1)}, u32[]{:S(2)}, u32[]{:S(2)}) collective-permute-start(bf16[256,1024]{1,0:T(8,128)(2,1)S(1)} %token_.1.grad_own), channel_id=1, source_target_pairs={{0,2},{2,0},{1,3},{3,1},{4,6},{6,4},{5,7},{7,5},{8,10},{10,8},{9,1... | collective-permute-start | bytes 1572872 | tf_op jit(solution)/shard_map/ppermute | solution.py:353
  69.6 1.6 %collective-permute-start.2 = (bf16[512,256]{1,0:T(8,128)(2,1)S(1)}, bf16[512,256]{1,0:T(8,128)(2,1)S(1)}, u32[]{:S(2)}, u32[]{:S(2)}) collective-permute-start(bf16[512,256]{1,0:T(8,128)(2,1)S(1)} %get-tuple-element.21), channel_id=1, source_target_pairs={{0,2},{2,0},{1,3},{3,1},{4,6},{6,4},{5,7},{7,5},{8,10},{10,8},{9,1... | collective-permute-start | bytes 786440 | tf_op jit(solution)/shard_map/ppermute | solution.py:320
  69.8 2.1 %collective-permute-start = (bf16[512,256]{1,0:T(8,128)(2,1)S(1)}, bf16[512,256]{1,0:T(8,128)(2,1)S(1)}, u32[]{:S(2)}, u32[]{:S(2)}) collective-permute-start(bf16[512,256]{1,0:T(8,128)(2,1)S(1)} %get-tuple-element.15), channel_id=1, source_target_pairs={{0,2},{2,0},{1,3},{3,1},{4,6},{6,4},{5,7},{7,5},{8,10},{10,8},{9,1... | collective-permute-start | bytes 786440 | tf_op jit(solution)/shard_map/ppermute | solution.py:319

commit v3 on v2

--- a/solution.py
+++ b/solution.py
@@ -42,15 +42,6 @@
 
 GELU_A = 0.7978845608028654
 GELU_B = 0.044715
-
-
-def fetch(pairs, sems):
-    copies = [
-        pltpu.make_async_copy(src, dst, sems.at[k]) for k, (src, dst) in enumerate(pairs)
-    ]
-    for copy in copies:
-        copy.start()
-    return copies
 
 
 def head_parts(j_ref, h):
@@ -87,56 +78,69 @@
 
 def front_kernel(
     counts, cotangent, pillar_proj, pillar_gain, latent_proj, input_proj, space_gain,
-    space_project, space_output, features, before, hidden, stream, joined, packed,
+    space_project, space_output, own, send, before, stream, joined, packed,
     w_pillar, w_latent, w_input, w_project, w_output, counted, mixed,
-    v_features, v_before, v_hidden, v_stream, v_joined, sems, out_sems,
+    v_turned, v_before, v_stream, v_joined, sems, out_sems,
 ):
-    copies = fetch(
-        [
-            (counts, counted),
-            (pillar_proj, w_pillar),
-            (latent_proj, w_latent),
-            (input_proj, w_input),
-            (space_project, w_project),
-            (space_output, w_output),
-            (cotangent.at[lax.axis_index("grp")], packed.at[:, 1]),
-        ],
-        sems,
-    )
+    core = lax.axis_index("core")
+    copies = [
+        pltpu.make_async_copy(src, dst, sems.at[k])
+        for k, (src, dst) in enumerate(
+            (
+                (counts, counted),
+                (pillar_proj, w_pillar),
+                (latent_proj, w_latent),
+                (input_proj, w_input),
+                (space_project.at[:, pl.ds(0, D)], w_project.at[:, pl.ds(0, D)]),
+                (space_output, w_output),
+                (cotangent.at[lax.axis_index("grp")], packed.at[:, 1]),
+                (space_project.at[:, pl.ds(D, D)], w_project.at[:, pl.ds(D, D)]),
+                (space_project.at[:, pl.ds(2 * D, D)], w_project.at[:, pl.ds(2 * D, D)]),
+            )
+        )
+    ]
     saves = [
         pltpu.make_async_copy(src, dst, out_sems.at[k])
         for k, (src, dst) in enumerate(
             (
-                (v_features, features),
+                (v_turned.at[:, core], own),
+                (v_turned.at[:, 1 - core], send),
                 (v_before, before),
-                (v_hidden, hidden),
                 (v_stream, stream),
                 (v_joined, joined),
             )
         )
     ]
+
+    def turn(values, k):
+        blocks = values.T.reshape(32, 2, 16, TOK)
+        v_turned[k, 0] = blocks[:, 0].reshape(512, TOK)
+        v_turned[k, 1] = blocks[:, 1].reshape(512, TOK)
+
+    for k in (0, 1, 2, 3, 4, 7, 8, 5, 6):
+        copies[k].start()
     copies[0].wait()
     x = jnp.log(counted[...].astype(F32) + 1.0).astype(BF16)
-    v_features[...] = x
-    saves[0].start()
     copies[1].wait()
     b = dot(x, w_pillar[...])
+    turn(x, 0)
     v_before[...] = b
-    saves[1].start()
+    saves[2].start()
     n = b * inverse_rms(b) * pillar_gain[...]
     hid = (0.5 * n * (1.0 + jnp.tanh(GELU_A * (n + GELU_B * n * n * n)))).astype(BF16)
-    v_hidden[...] = hid
-    saves[2].start()
     copies[2].wait()
     lat = dot(hid, w_latent[...]).astype(BF16)
+    turn(hid, 1)
+    saves[0].start()
+    saves[1].start()
     copies[3].wait()
     s = dot(lat, w_input[...]).astype(BF16)
     v_stream[...] = s
     saves[3].start()
     s = s.astype(F32)
     u = (s * inverse_rms(s) * space_gain[...]).astype(BF16)
-    copies[4].wait()
-    for part in range(3):
+    for part, k in enumerate((4, 7, 8)):
+        copies[k].wait()
         cols = slice(part * D, (part + 1) * D)
         v_joined[:, cols] = dot(u, w_project[:, cols]).astype(BF16)
     saves[4].start()
@@ -154,14 +158,6 @@
     copies[6].wait()
     for save in saves:
         save.wait()
-
-
-def turn_kernel(features, hidden, feat_own, feat_send, hid_own, hid_send, turned):
-    core = lax.axis_index("core")
-    for src, own, send in ((features, feat_own, feat_send), (hidden, hid_own, hid_send)):
-        turned[...] = src[...].T.reshape(32, 2, 16, TOK)
-        own[...] = turned[:, core].reshape(512, TOK)
-        send[...] = turned[:, 1 - core].reshape(512, TOK)
 
 
 def time_kernel(
@@ -173,14 +169,13 @@
     e = col // FRAMES
     seen = (row % FRAMES == col % FRAMES) & (e <= row // FRAMES) & (e < valid)
     masked[...] = seen.astype(F32)
-    cot = packed[:, 1].reshape(TOK, D)
-    dmixed[...] = dot_nt(cot, w_output[...]).astype(BF16)
     s = packed[:, 0].reshape(TOK, D).astype(F32)
     inverse = inverse_rms(s)
     u = (s * inverse * time_gain[...]).astype(BF16)
     for part in range(3):
         cols = slice(part * D, (part + 1) * D)
         joined[:, cols] = dot(u, w_project[:, cols]).astype(BF16)
+    dmixed[...] = dot_nt(packed[:, 1].reshape(TOK, D), w_output[...]).astype(BF16)
 
     def head(h, carry):
         attention_back(joined, dmixed, djoined, masked[...], h)
@@ -221,11 +216,12 @@
 
 
 def latent_kernel(own, other, grad_own, grad_other, out):
-    out[...] = (dot(own[...], grad_own[...]) + dot(other[...], grad_other[...])).astype(BF16)
+    part = dot(own[1], grad_own[...]) + dot(other[1], grad_other[...])
+    out[...] = part.astype(BF16)
 
 
 def pillar_kernel(own, other, grad_own, grad_other, latent, out):
-    part = dot(own[...], grad_own[...]) + dot(other[...], grad_other[...])
+    part = dot(own[0], grad_own[...]) + dot(other[0], grad_other[...])
     out[:, 0] = part.reshape(64, 8, D).astype(BF16)
     out[:, 1] = latent[...].reshape(64, 8, D)
 
@@ -257,6 +253,8 @@
 
 UNIT = 2 * TOK * D * D
 MIB = 1 << 20
+FRONT_LIMIT = 52 * MIB
+TIME_LIMIT = 28 * MIB
 
 
 def shards(
@@ -284,12 +282,13 @@
     def exchange(values, axes):
         return lax.all_to_all(values, axes, split_axis=0, concat_axis=0, tiled=True)
 
+    half = struct((2, 512, TOK), BF16)
     wide = lambda n, dtype=BF16: pltpu.VMEM((D, n * D), dtype)
     tall = lambda n, dtype=BF16: pltpu.VMEM((TOK, n * D), dtype)
-    features, before, hidden, stream, joined, packed = call(
+    own, send, before, stream, joined, packed = call(
         front_kernel,
         "front",
-        (rows, struct((TOK, D), F32), rows, rows, struct((TOK, 3 * D), BF16),
+        (half, half, struct((TOK, D), F32), rows, struct((TOK, 3 * D), BF16),
          struct((16, 2, 16, D), BF16)),
         [HBM, HBM, HBM, VMEM, HBM, HBM, VMEM, HBM, HBM],
         (
@@ -297,27 +296,14 @@
             latent_proj, input_proj, space_gain, space_project, space_output,
         ),
         [wide(1), wide(1), wide(1), wide(3), wide(1), tall(1, jnp.int32), tall(1),
-         tall(1), tall(1, F32), tall(1), tall(1), tall(3),
-         pltpu.SemaphoreType.DMA((7,)), pltpu.SemaphoreType.DMA((5,))],
+         pltpu.VMEM((2, 2, 512, TOK), BF16), tall(1, F32), tall(1), tall(3),
+         pltpu.SemaphoreType.DMA((9,)), pltpu.SemaphoreType.DMA((5,))],
         8 * UNIT,
         20 * MIB,
-        None,
+        FRONT_LIMIT,
         [HBM, HBM, HBM, HBM, HBM, VMEM],
     )
     packed = exchange(packed, scene)
-    half = struct((512, TOK), BF16)
-    feat_own, feat_send, hid_own, hid_send = call(
-        turn_kernel,
-        "turn",
-        (half, half, half, half),
-        [VMEM, VMEM],
-        (features, hidden),
-        [pltpu.VMEM((32, 2, 16, TOK), BF16)],
-        0,
-        2 * MIB,
-    )
-    feat_other = lax.ppermute(feat_send, "core", swap)
-    hid_other = lax.ppermute(hid_send, "core", swap)
     grad_tok = call(
         time_kernel,
         "time",
@@ -327,6 +313,7 @@
         [tall(3), tall(1), tall(3), pltpu.VMEM((TOK, TOK), F32)],
         9 * UNIT,
         10 * MIB,
+        TIME_LIMIT,
     )
     dspaced = exchange(grad_tok, scene)
     dlatent = call(
@@ -339,6 +326,8 @@
         7 * UNIT,
         14 * MIB,
     )
+    dlatent, send = lax.optimization_barrier((dlatent, send))
+    other = lax.ppermute(send, "core", swap)
     dlatent_other = lax.ppermute(dlatent, "core", swap)
     dbefore = call(
         token_kernel,
@@ -353,11 +342,11 @@
     dbefore_other = lax.ppermute(dbefore, "core", swap)
     latent_part = call(
         latent_kernel, "latent_weight", struct((512, D), BF16), [VMEM] * 4,
-        (hid_own, hid_other, dlatent, dlatent_other), (), UNIT, 2 * MIB,
+        (own, other, dlatent, dlatent_other), (), UNIT, 2 * MIB,
     )
     parts = call(
         pillar_kernel, "pillar_weight", struct((64, 2, 8, D), BF16), [VMEM] * 5,
-        (feat_own, feat_other, dbefore, dbefore_other, latent_part), (), UNIT, 4 * MIB,
+        (own, other, dbefore, dbefore_other, latent_part), (), UNIT, 4 * MIB,
     )
     parts = exchange(parts, ("grp", "x", "z", "dp"))
     out = struct((8, D), F32)

time: 113 us -> 109 us (0.965)
  Pallas kernels: 32.1 us -> 30.2 us
  local copies, waits for them, and re-layouts: 2.86 us -> 1.44 us
    pallas_call x8 -> x7, Pallas kernels: 32.1 us -> 30.2 us  [call(): pl.pallas_call(kernel, out_shape=outs, in_specs=in_specs, out_specs=out_s...]
    unnamed x32 -> x28, local copies, waits for them, and re-layouts: 2.86 us -> 1.44 us
  transfers between devices with their start and end apart: 4 -> 3, of which waited for: 1 -> 2; matrix products, arithmetic and copies ran while one was open for 0% -> 0% of each run, Pallas kernels for 2% -> 2%
where the time goes in v3:
time: 109 us; the launch traced here: 108 us
  blocking collectives  74.1 us (68%)
  Pallas kernels  30.2 us (28%)
  local copies, waits for them, and re-layouts  1.44 us (1%)
    all_to_all x3, blocking collectives, exchange(): return lax.all_to_all(values, axes, split_axis=0, concat_axis=0, tiled=True)  74.1 us
    pallas_call x7, Pallas kernels, call(): pl.pallas_call(kernel, out_shape=outs, in_specs=in_specs, out_specs=out_s...  30.2 us
  transfers between devices with their start and end apart: 3, of which 2 were waited for; matrix products, arithmetic and copies ran while one was open for 0% of the time, Pallas kernels for 2%

profile of v3, /device:TPU:0, one launch (start us, length us, event | category | flops | bytes accessed | tf_op | source)
XLA Modules:
  0.0 108.4 jit_solution(6335493246265065570)
XLA Ops:
  0.6 0.0 copy-start.4
  0.6 0.7 copy-done.4
  1.3 0.7 copy-done.6
  2.0 9.9 %front.1 = (bf16[2,512,256]{2,1,0:T(8,128)(2,1)S(1)}, bf16[2,512,256]{2,1,0:T(8,128)(2,1)S(1)}, f32[256,1024]{1,0:T(8,128)}, bf16[256,1024]{1,0:T(8,128)(2,1)S(1...) custom-call(s32[256,1024]{1,0:T(8,128)} %bitcast.16, bf16[2,16,16,1024]{3,2,1,0:T(8,128)(2,1)} %bitcast.17, ...), custom_call_target="tpu_custom_call" | custom-call | flops 4294967296 | bytes 20971520 | tf_op jit(solution)/shard_map/front/pallas_call | solution.py:240
  11.9 0.0 copy-start.8
  11.9 0.0 slice-start
  11.9 22.3 %all_to_all.21.packed = bf16[16,2,16,1024]{3,2,1,0:T(8,128)(2,1)S(1)} all-to-all(bf16[16,2,16,1024]{3,2,1,0:T(8,128)(2,1)} %get-tuple-element.11), channel_id=1, replica_groups=mesh['grp'=2,'x'=4,'z'=4,'core'=2,'dp'=2] {'z','core','grp'}, dimensions={0} | all-to-all | bytes 2097152 | tf_op jit(solution)/shard_map/all_to_all | solution.py:283
  34.2 0.0 slice-start.1
  34.3 0.0 copy-start.1
  34.3 9.1 %time.1 = bf16[256,1024]{1,0:T(8,128)(2,1)S(1)} custom-call(s32[2,4]{1,0:T(2,128)S(1)} %copy-done.11, bf16[16,2,16,1024]{3,2,1,0:T(8,128)(2,1)S(1)} %all_to_all.21.packed, f32[1,1024]{1,0:T(1,128)S(1)} %bitcast.15, bf16[1024,3072]{1,0:T(8,128)(2,1)S(1)} %copy-done.7, bf16[1024,1024]{1,0:T(8,128)(2,1)S(1)} %copy-done.8), custom_call_target="tpu_custom_call" | custom-call | flops 4831838208 | bytes 10485760 | tf_op jit(solution)/shard_map/time/pallas_call | solution.py:240
  43.4 13.2 %all_to_all.22 = bf16[16,16,1024]{2,1,0:T(8,128)(2,1)S(1)} all-to-all(bf16[16,16,1024]{2,1,0:T(8,128)(2,1)S(1)} %bitcast.10), channel_id=1, replica_groups=mesh['grp'=2,'x'=4,'z'=4,'core'=2,'dp'=2] {'z','core','grp'}, dimensions={0} | all-to-all | bytes 1048576 | tf_op jit(solution)/shard_map/all_to_all | solution.py:283
  56.7 0.0 copy-start
  56.7 0.0 copy-start.5
  56.7 7.3 %back.1.dlatent.grad_own = bf16[256,1024]{1,0:T(8,128)(2,1)S(1)} custom-call(bf16[256,1024]{1,0:T(8,128)(2,1)S(1)} %bitcast.9, bf16[256,3072]{1,0:T(8,128)(2,1)S(1)} %copy-done.9, bf16[256,1024]{1,0:T(8,128)(2,1)S(1)} %get-tuple-element.13.stream, f32[1,1024]{1,0:T(1,128)S(1)} %bitcast.14, bf16[1024,1024]{1,0:T(8,128)(2,1)S(1)} %copy-done.2, ...), custom_call_target="tpu_custom_call" | custom-call | flops 3758096384 | bytes 14680064 | tf_op jit(solution)/shard_map/back/pallas_call | solution.py:240
  64.0 0.3 collective-permute-start
  64.3 0.3 collective-permute-start.2
  64.6 1.5 %token_.1.grad_own = bf16[256,1024]{1,0:T(8,128)(2,1)S(1)} custom-call(bf16[256,1024]{1,0:T(8,128)(2,1)S(1)} %back.1.dlatent.grad_own, f32[256,1024]{1,0:T(8,128)S(1)} %copy-done.3, f32[1,1024]{1,0:T(1,128)S(1)} %bitcast.12, bf16[1024,1024]{1,0:T(8,128)(2,1)S(1)} %copy-done), custom_call_target="tpu_custom_call" | custom-call | flops 536870912 | bytes 4194304 | tf_op jit(solution)/shard_map/token/pallas_call | solution.py:240
  66.2 0.3 collective-permute-start.1
  66.4 0.4 collective-permute-done.2.grad_other
  66.8 0.7 latent_weight.1.latent
  67.5 0.7 collective-permute-done.1.grad_other
  68.2 0.7 pillar_weight.1
  68.9 38.6 %all_to_all.23.parts = bf16[64,2,8,1024]{3,2,1,0:T(8,128)(2,1)S(1)} all-to-all(bf16[64,2,8,1024]{3,2,1,0:T(8,128)(2,1)S(1)} %pillar_weight.1), channel_id=1, replica_groups=mesh['grp'=2,'x'=4,'z'=4,'core'=2,'dp'=2] {'grp','x','z','dp'}, dimensions={0} | all-to-all | bytes 4194304 | tf_op jit(solution)/shard_map/all_to_all | solution.py:283
  107.4 0.9 total.1
  (21 shorter events, 0.0 us)
Async XLA Ops:
  0.6 0.7 copy-start.4
  1.3 0.7 copy-start.6
  2.0 32.2 %copy-start.7 = (bf16[1024,3072]{1,0:T(8,128)(2,1)S(1)}, bf16[1024,3072]{1,0:T(8,128)(2,1)}, u32[]{:S(2)}) copy-start(bf16[1024,3072]{1,0:T(8,128)(2,1)} %w_project.2) | copy-start | bytes 18874372
  2.0 32.2 %copy-start.10 = (f32[1024]{0:T(1024)S(1)}, f32[1024]{0:T(1024)}, u32[]{:S(2)}) copy-start(f32[1024]{0:T(1024)} %param.23) | copy-start | bytes 12292
  11.9 22.3 %copy-start.8 = (bf16[1024,1024]{1,0:T(8,128)(2,1)S(1)}, bf16[1024,1024]{1,0:T(8,128)(2,1)}, u32[]{:S(2)}) copy-start(bf16[1024,1024]{1,0:T(8,128)(2,1)} %w_output.2) | copy-start | bytes 6291460
  11.9 22.3 %copy-start.11 = (s32[2,4]{1,0:T(2,128)S(1)}, s32[2,4]{1,0:T(2,128)}, u32[]{:S(2)}) copy-start(s32[2,4]{1,0:T(2,128)} %valid_frames.1) | copy-start | bytes 100
  11.9 44.7 %slice-start = ((s8[6291456]{0:T(1024)(128)(4,1)}), s8[4194304]{0:T(1024)(128)(4,1)S(1)}, s32[]{:S(2)}) async-start(s8[6291456]{0:T(1024)(128)(4,1)} %bitcast.7), calls=%async_computation.3 | async-start | bytes 8388608
  34.2 22.4 %slice-start.1 = ((s8[6291456]{0:T(1024)(128)(4,1)}), s8[2097152]{0:T(1024)(128)(4,1)S(1)}, s32[]{:S(2)}) async-start(s8[6291456]{0:T(1024)(128)(4,1)} %bitcast.7), calls=%async_computation.4 | async-start | bytes 4194304
  34.3 22.4 %copy-start.1 = (bf16[1024,1024]{1,0:T(8,128)(2,1)S(1)}, bf16[1024,1024]{1,0:T(8,128)(2,1)}, u32[]{:S(2)}) copy-start(bf16[1024,1024]{1,0:T(8,128)(2,1)} %w_input.1) | copy-start | bytes 6291460
  34.3 22.4 %copy-start.2 = (bf16[1024,1024]{1,0:T(8,128)(2,1)S(1)}, bf16[1024,1024]{1,0:T(8,128)(2,1)}, u32[]{:S(2)}) copy-start(bf16[1024,1024]{1,0:T(8,128)(2,1)} %w_output.3) | copy-start | bytes 6291460
  34.3 22.4 %copy-start.9 = (bf16[256,3072]{1,0:T(8,128)(2,1)S(1)}, bf16[256,3072]{1,0:T(8,128)(2,1)}, u32[]{:S(2)}) copy-start(bf16[256,3072]{1,0:T(8,128)(2,1)} %get-tuple-element.12.joined) | copy-start | bytes 4718596
  56.7 8.0 %copy-start = (bf16[1024,1024]{1,0:T(8,128)(2,1)S(1)}, bf16[1024,1024]{1,0:T(8,128)(2,1)}, u32[]{:S(2)}) copy-start(bf16[1024,1024]{1,0:T(8,128)(2,1)} %latent_proj.3) | copy-start | bytes 6291460
  56.7 8.0 %copy-start.3 = (f32[256,1024]{1,0:T(8,128)S(1)}, f32[256,1024]{1,0:T(8,128)}, u32[]{:S(2)}) copy-start(f32[256,1024]{1,0:T(8,128)} %get-tuple-element.17.before) | copy-start | bytes 3145732
  56.7 8.0 %copy-start.5 = (f32[1024]{0:T(1024)S(1)}, f32[1024]{0:T(1024)}, u32[]{:S(2)}) copy-start(f32[1024]{0:T(1024)} %param.17) | copy-start | bytes 12292
  64.0 2.4 %collective-permute-start = (bf16[2,512,256]{2,1,0:T(8,128)(2,1)S(1)}, bf16[2,512,256]{2,1,0:T(8,128)(2,1)S(1)}, u32[]{:S(2)}, u32[]{:S(2)}) collective-permute-start(bf16[2,512,256]{2,1,0:T(8,128)(2,1)S(1)} %get-tuple-element.15), channel_id=1, source_target_pairs={{0,2},{2,0},{1,3},{3,1},{4,6},{6,4},{5,7},{7,5},{8,10},{10,8},{9,1... | collective-permute-start | bytes 1572872 | tf_op jit(solution)/shard_map/ppermute | solution.py:330
  64.3 2.5 %collective-permute-start.2 = (bf16[256,1024]{1,0:T(8,128)(2,1)S(1)}, bf16[256,1024]{1,0:T(8,128)(2,1)S(1)}, u32[]{:S(2)}, u32[]{:S(2)}) collective-permute-start(bf16[256,1024]{1,0:T(8,128)(2,1)S(1)} %back.1.dlatent.grad_own), channel_id=1, source_target_pairs={{0,2},{2,0},{1,3},{3,1},{4,6},{6,4},{5,7},{7,5},{8,10},{10,8},{9,1... | collective-permute-start | bytes 1572872 | tf_op jit(solution)/shard_map/ppermute | solution.py:331
  66.2 2.0 %collective-permute-start.1 = (bf16[256,1024]{1,0:T(8,128)(2,1)S(1)}, bf16[256,1024]{1,0:T(8,128)(2,1)S(1)}, u32[]{:S(2)}, u32[]{:S(2)}) collective-permute-start(bf16[256,1024]{1,0:T(8,128)(2,1)S(1)} %token_.1.grad_own), channel_id=1, source_target_pairs={{0,2},{2,0},{1,3},{3,1},{4,6},{6,4},{5,7},{7,5},{8,10},{10,8},{9,1... | collective-permute-start | bytes 1572872 | tf_op jit(solution)/shard_map/ppermute | solution.py:342

commit v4 on v3

--- a/solution.py
+++ b/solution.py
@@ -14,6 +14,7 @@
 F32 = jnp.float32
 BF16 = jnp.bfloat16
 SCALE = HEAD**-0.5
+SCALE_LOG2E = SCALE * 1.4426950408889634
 VMEM = pl.BlockSpec(memory_space=pltpu.VMEM)
 SMEM = pl.BlockSpec(memory_space=pltpu.SMEM)
 HBM = pl.BlockSpec(memory_space=pltpu.HBM)
@@ -54,10 +55,10 @@
 
 
 def softmax(qn, kn, mask):
-    w = jnp.exp(dot_nt(qn, kn) * SCALE)
+    w = jnp.exp2(dot_nt(qn, kn) * SCALE_LOG2E)
     if mask is not None:
         w = w * mask
-    return w / jnp.sum(w, axis=-1, keepdims=True)
+    return w * (1.0 / jnp.sum(w, axis=-1, keepdims=True))
 
 
 def attention_back(j_ref, dm_ref, dj_ref, mask, h):
@@ -67,18 +68,18 @@
     dm = dm_ref[:, cols]
     dp = dot_nt(dm, v).astype(BF16).astype(F32)
     dv = dot_tn(weights.astype(BF16), dm)
-    ds = weights * (dp - jnp.sum(dp * weights, axis=-1, keepdims=True)) * SCALE
+    ds = weights * (dp - jnp.sum(dp * weights, axis=-1, keepdims=True))
     ds = ds.astype(BF16)
-    dqn = dot(ds, kn).astype(BF16).astype(F32)
-    dkn = dot_tn(ds, qn).astype(BF16).astype(F32)
+    dqn = (dot(ds, kn) * SCALE).astype(BF16).astype(F32)
+    dkn = (dot_tn(ds, qn) * SCALE).astype(BF16).astype(F32)
     dj_ref[:, cols] = norm_back(q, iq, dqn).astype(BF16)
     dj_ref[:, pl.ds(pl.multiple_of(D + h * HEAD, HEAD), HEAD)] = norm_back(k, ik, dkn).astype(BF16)
     dj_ref[:, pl.ds(pl.multiple_of(2 * D + h * HEAD, HEAD), HEAD)] = dv.astype(BF16)
 
 
 def front_kernel(
-    counts, cotangent, pillar_proj, pillar_gain, latent_proj, input_proj, space_gain,
-    space_project, space_output, own, send, before, stream, joined, packed,
+    counts, cotangent, pillar_proj, gains, latent_proj, input_proj, space_project,
+    space_output, own, send, before, stream, joined, packed,
     w_pillar, w_latent, w_input, w_project, w_output, counted, mixed,
     v_turned, v_before, v_stream, v_joined, sems, out_sems,
 ):
@@ -126,7 +127,7 @@
     turn(x, 0)
     v_before[...] = b
     saves[2].start()
-    n = b * inverse_rms(b) * pillar_gain[...]
+    n = b * inverse_rms(b) * gains[0:1]
     hid = (0.5 * n * (1.0 + jnp.tanh(GELU_A * (n + GELU_B * n * n * n)))).astype(BF16)
     copies[2].wait()
     lat = dot(hid, w_latent[...]).astype(BF16)
@@ -138,7 +139,7 @@
     v_stream[...] = s
     saves[3].start()
     s = s.astype(F32)
-    u = (s * inverse_rms(s) * space_gain[...]).astype(BF16)
+    u = (s * inverse_rms(s) * gains[1:2]).astype(BF16)
     for part, k in enumerate((4, 7, 8)):
         copies[k].wait()
         cols = slice(part * D, (part + 1) * D)
@@ -161,7 +162,7 @@
 
 
 def time_kernel(
-    valid_frames, packed, time_gain, w_project, w_output, grad, joined, dmixed, djoined, masked
+    valid_frames, packed, gains, w_project, w_output, grad, joined, dmixed, djoined, masked
 ):
     valid = valid_frames[lax.axis_index("dp"), lax.axis_index("x")]
     row = lax.broadcasted_iota(jnp.int32, (TOK, TOK), 0)
@@ -171,7 +172,7 @@
     masked[...] = seen.astype(F32)
     s = packed[:, 0].reshape(TOK, D).astype(F32)
     inverse = inverse_rms(s)
-    u = (s * inverse * time_gain[...]).astype(BF16)
+    u = (s * inverse * gains[2:3]).astype(BF16)
     for part in range(3):
         cols = slice(part * D, (part + 1) * D)
         joined[:, cols] = dot(u, w_project[:, cols]).astype(BF16)
@@ -182,14 +183,14 @@
         return carry
 
     lax.fori_loop(0, HEADS, head, 0, unroll=True)
-    du = dot_nt(djoined[...], w_project[...]).astype(BF16).astype(F32) * time_gain[...]
+    du = dot_nt(djoined[...], w_project[...]).astype(BF16).astype(F32) * gains[2:3]
     s = packed[:, 0].reshape(TOK, D).astype(F32)
     cot = packed[:, 1].reshape(TOK, D).astype(F32)
     grad[...] = (cot + norm_back(s, inverse_rms(s), du)).astype(BF16)
 
 
 def back_kernel(
-    dspaced, joined, stream, space_gain, w_output, w_project, w_input, dlatent, dmixed, djoined
+    dspaced, joined, stream, gains, w_output, w_project, w_input, dlatent, dmixed, djoined
 ):
     dmixed[...] = dot_nt(dspaced[...], w_output[...]).astype(BF16)
 
@@ -198,20 +199,20 @@
         return carry
 
     lax.fori_loop(0, HEADS, head, 0, unroll=True)
-    du = dot_nt(djoined[...], w_project[...]).astype(BF16).astype(F32) * space_gain[...]
+    du = dot_nt(djoined[...], w_project[...]).astype(BF16).astype(F32) * gains[1:2]
     s = stream[...].astype(F32)
     dstream = (dspaced[...].astype(F32) + norm_back(s, inverse_rms(s), du)).astype(BF16)
     dlatent[...] = dot_nt(dstream, w_input[...]).astype(BF16)
 
 
-def token_kernel(dlatent, before, pillar_gain, latent_proj, dbefore):
+def token_kernel(dlatent, before, gains, latent_proj, dbefore):
     dhid = dot_nt(dlatent[...], latent_proj[...])
     b = before[...]
     inverse = inverse_rms(b)
-    n = b * inverse * pillar_gain[...]
+    n = b * inverse * gains[0:1]
     t = jnp.tanh(GELU_A * (n + GELU_B * n * n * n))
     slope = 0.5 * (1.0 + t) + 0.5 * n * (1.0 - t * t) * (GELU_A * (1.0 + 3.0 * GELU_B * n * n))
-    dn = dhid * slope * pillar_gain[...]
+    dn = dhid * slope * gains[0:1]
     dbefore[...] = norm_back(b, inverse, dn).astype(BF16)
 
 
@@ -275,9 +276,7 @@
     rows = struct((TOK, D), BF16)
     scene = ("z", "core", "grp")
     swap = ((0, 1), (1, 0))
-    pillar_gain = pillar_gain.reshape(1, D)
-    space_gain = space_gain.reshape(1, D)
-    time_gain = time_gain.reshape(1, D)
+    gains = jnp.stack([pillar_gain, space_gain, time_gain])
 
     def exchange(values, axes):
         return lax.all_to_all(values, axes, split_axis=0, concat_axis=0, tiled=True)
@@ -290,10 +289,10 @@
         "front",
         (half, half, struct((TOK, D), F32), rows, struct((TOK, 3 * D), BF16),
          struct((16, 2, 16, D), BF16)),
-        [HBM, HBM, HBM, VMEM, HBM, HBM, VMEM, HBM, HBM],
+        [HBM, HBM, HBM, VMEM, HBM, HBM, HBM, HBM],
         (
-            counts.reshape(TOK, D), cotangent.reshape(2, 16, 16, D), pillar_proj, pillar_gain,
-            latent_proj, input_proj, space_gain, space_project, space_output,
+            counts.reshape(TOK, D), cotangent.reshape(2, 16, 16, D), pillar_proj, gains,
+            latent_proj, input_proj, space_project, space_output,
         ),
         [wide(1), wide(1), wide(1), wide(3), wide(1), tall(1, jnp.int32), tall(1),
          pltpu.VMEM((2, 2, 512, TOK), BF16), tall(1, F32), tall(1), tall(3),
@@ -309,7 +308,7 @@
         "time",
         rows,
         [SMEM, VMEM, VMEM, VMEM, VMEM],
-        (valid_frames, packed, time_gain, time_project, time_output),
+        (valid_frames, packed, gains, time_project, time_output),
         [tall(3), tall(1), tall(3), pltpu.VMEM((TOK, TOK), F32)],
         9 * UNIT,
         10 * MIB,
@@ -321,7 +320,7 @@
         "back",
         rows,
         [VMEM] * 7,
-        (dspaced, joined, stream, space_gain, space_output, space_project, input_proj),
+        (dspaced, joined, stream, gains, space_output, space_project, input_proj),
         [tall(1), tall(3)],
         7 * UNIT,
         14 * MIB,
@@ -334,7 +333,7 @@
         "token",
         rows,
         [VMEM, VMEM, VMEM, VMEM],
-        (dlatent, before, pillar_gain, latent_proj),
+        (dlatent, before, gains, latent_proj),
         (),
         UNIT,
         4 * MIB,

time: 109 us -> 108 us (level)
  local copies, waits for them, and re-layouts: 1.44 us -> 0.06 us
    unnamed x28 -> x20, local copies, waits for them, and re-layouts: 1.44 us -> 0.06 us
where the time goes in v4:
time: 108 us; the launch traced here: 107 us
  blocking collectives  74.1 us (69%)
  Pallas kernels  29.8 us (28%)
    all_to_all x3, blocking collectives, exchange(): return lax.all_to_all(values, axes, split_axis=0, concat_axis=0, tiled=True)  74.1 us
    pallas_call x7, Pallas kernels, call(): pl.pallas_call(kernel, out_shape=outs, in_specs=in_specs, out_specs=out_s...  29.8 us
  transfers between devices with their start and end apart: 3, of which 2 were waited for; matrix products, arithmetic and copies ran while one was open for 0% of the time, Pallas kernels for 2%

profile of v4, /device:TPU:0, one launch (start us, length us, event | category | flops | bytes accessed | tf_op | source)
XLA Modules:
  0.0 107.3 jit_solution(15119473472320808292)
XLA Ops:
  0.6 0.7 pad_maximum_fusion.gains
  1.4 0.0 copy-start.4
  1.4 9.8 %front.1 = (bf16[2,512,256]{2,1,0:T(8,128)(2,1)S(1)}, bf16[2,512,256]{2,1,0:T(8,128)(2,1)S(1)}, f32[256,1024]{1,0:T(8,128)}, bf16[256,1024]{1,0:T(8,128)(2,1)S(1...) custom-call(s32[256,1024]{1,0:T(8,128)} %bitcast.11, bf16[2,16,16,1024]{3,2,1,0:T(8,128)(2,1)} %bitcast.12, ...), custom_call_target="tpu_custom_call" | custom-call | flops 4294967296 | bytes 20971520 | tf_op jit(solution)/shard_map/front/pallas_call | solution.py:241
  11.2 0.0 copy-start.5
  11.2 0.0 copy-start.7
  11.3 0.0 slice-start
  11.3 22.3 %all_to_all.21.packed = bf16[16,2,16,1024]{3,2,1,0:T(8,128)(2,1)S(1)} all-to-all(bf16[16,2,16,1024]{3,2,1,0:T(8,128)(2,1)} %get-tuple-element.11), channel_id=1, replica_groups=mesh['grp'=2,'x'=4,'z'=4,'core'=2,'dp'=2] {'z','core','grp'}, dimensions={0} | all-to-all | bytes 2097152 | tf_op jit(solution)/shard_map/all_to_all | solution.py:282
  33.6 0.0 slice-start.1
  33.6 0.0 copy-start.1
  33.6 0.0 copy-start.2
  33.6 9.0 %time.1 = bf16[256,1024]{1,0:T(8,128)(2,1)S(1)} custom-call(s32[2,4]{1,0:T(2,128)S(1)} %copy-done.7, bf16[16,2,16,1024]{3,2,1,0:T(8,128)(2,1)S(1)} %all_to_all.21.packed, f32[3,1024]{1,0:T(4,128)S(1)} %pad_maximum_fusion.gains, bf16[1024,3072]{1,0:T(8,128)(2,1)S(1)} %copy-done.4, bf16[1024,1024]{1,0:T(8,128)(2,1)S(1)} %copy-done.5), custom_call_target="tpu_custom_call" | custom-call | flops 4831838208 | bytes 10485760 | tf_op jit(solution)/shard_map/time/pallas_call | solution.py:241
  42.6 13.2 %all_to_all.22 = bf16[16,16,1024]{2,1,0:T(8,128)(2,1)S(1)} all-to-all(bf16[16,16,1024]{2,1,0:T(8,128)(2,1)S(1)} %bitcast.10), channel_id=1, replica_groups=mesh['grp'=2,'x'=4,'z'=4,'core'=2,'dp'=2] {'z','core','grp'}, dimensions={0} | all-to-all | bytes 1048576 | tf_op jit(solution)/shard_map/all_to_all | solution.py:282
  55.8 0.0 copy-start
  55.9 7.1 %back.1.dlatent.grad_own = bf16[256,1024]{1,0:T(8,128)(2,1)S(1)} custom-call(bf16[256,1024]{1,0:T(8,128)(2,1)S(1)} %bitcast.9, bf16[256,3072]{1,0:T(8,128)(2,1)S(1)} %copy-done.6, bf16[256,1024]{1,0:T(8,128)(2,1)S(1)} %get-tuple-element.13.stream, f32[3,1024]{1,0:T(4,128)S(1)} %pad_maximum_fusion.gains, bf16[1024,1024]{1,0:T(8,128)(2,1)S(1)} %copy-done.2, ...), custom_call_target="tpu_custom_call" | custom-call | flops 3758096384 | bytes 14680064 | tf_op jit(solution)/shard_map/back/pallas_call | solution.py:241
  63.0 0.3 collective-permute-start
  63.3 0.3 collective-permute-start.2
  63.6 1.5 %token_.1.grad_own = bf16[256,1024]{1,0:T(8,128)(2,1)S(1)} custom-call(bf16[256,1024]{1,0:T(8,128)(2,1)S(1)} %back.1.dlatent.grad_own, f32[256,1024]{1,0:T(8,128)S(1)} %copy-done.3, f32[3,1024]{1,0:T(4,128)S(1)} %pad_maximum_fusion.gains, bf16[1024,1024]{1,0:T(8,128)(2,1)S(1)} %copy-done), custom_call_target="tpu_custom_call" | custom-call | flops 536870912 | bytes 4194304 | tf_op jit(solution)/shard_map/token/pallas_call | solution.py:241
  65.1 0.3 collective-permute-start.1
  65.4 0.4 collective-permute-done.2.grad_other
  65.8 0.7 latent_weight.1.latent
  66.5 0.6 collective-permute-done.1.grad_other
  67.1 0.7 pillar_weight.1
  67.8 38.6 %all_to_all.23.parts = bf16[64,2,8,1024]{3,2,1,0:T(8,128)(2,1)S(1)} all-to-all(bf16[64,2,8,1024]{3,2,1,0:T(8,128)(2,1)S(1)} %pillar_weight.1), channel_id=1, replica_groups=mesh['grp'=2,'x'=4,'z'=4,'core'=2,'dp'=2] {'grp','x','z','dp'}, dimensions={0} | all-to-all | bytes 4194304 | tf_op jit(solution)/shard_map/all_to_all | solution.py:282
  106.4 0.9 total.1
  (14 shorter events, 0.0 us)
Async XLA Ops:
  1.4 32.2 %copy-start.4 = (bf16[1024,3072]{1,0:T(8,128)(2,1)S(1)}, bf16[1024,3072]{1,0:T(8,128)(2,1)}, u32[]{:S(2)}) copy-start(bf16[1024,3072]{1,0:T(8,128)(2,1)} %w_project.2) | copy-start | bytes 18874372
  11.2 22.4 %copy-start.5 = (bf16[1024,1024]{1,0:T(8,128)(2,1)S(1)}, bf16[1024,1024]{1,0:T(8,128)(2,1)}, u32[]{:S(2)}) copy-start(bf16[1024,1024]{1,0:T(8,128)(2,1)} %w_output.2) | copy-start | bytes 6291460
  11.2 22.3 %copy-start.7 = (s32[2,4]{1,0:T(2,128)S(1)}, s32[2,4]{1,0:T(2,128)}, u32[]{:S(2)}) copy-start(s32[2,4]{1,0:T(2,128)} %valid_frames.1) | copy-start | bytes 100
  11.3 44.5 %slice-start = ((s8[6291456]{0:T(1024)(128)(4,1)}), s8[4194304]{0:T(1024)(128)(4,1)S(1)}, s32[]{:S(2)}) async-start(s8[6291456]{0:T(1024)(128)(4,1)} %bitcast.7), calls=%async_computation.3 | async-start | bytes 8388608
  33.6 22.2 %slice-start.1 = ((s8[6291456]{0:T(1024)(128)(4,1)}), s8[2097152]{0:T(1024)(128)(4,1)S(1)}, s32[]{:S(2)}) async-start(s8[6291456]{0:T(1024)(128)(4,1)} %bitcast.7), calls=%async_computation.4 | async-start | bytes 4194304
  33.6 22.2 %copy-start.1 = (bf16[1024,1024]{1,0:T(8,128)(2,1)S(1)}, bf16[1024,1024]{1,0:T(8,128)(2,1)}, u32[]{:S(2)}) copy-start(bf16[1024,1024]{1,0:T(8,128)(2,1)} %w_input.1) | copy-start | bytes 6291460
  33.6 22.2 %copy-start.2 = (bf16[1024,1024]{1,0:T(8,128)(2,1)S(1)}, bf16[1024,1024]{1,0:T(8,128)(2,1)}, u32[]{:S(2)}) copy-start(bf16[1024,1024]{1,0:T(8,128)(2,1)} %w_output.3) | copy-start | bytes 6291460
  33.6 22.2 %copy-start.6 = (bf16[256,3072]{1,0:T(8,128)(2,1)S(1)}, bf16[256,3072]{1,0:T(8,128)(2,1)}, u32[]{:S(2)}) copy-start(bf16[256,3072]{1,0:T(8,128)(2,1)} %get-tuple-element.12.joined) | copy-start | bytes 4718596
  55.8 7.8 %copy-start = (bf16[1024,1024]{1,0:T(8,128)(2,1)S(1)}, bf16[1024,1024]{1,0:T(8,128)(2,1)}, u32[]{:S(2)}) copy-start(bf16[1024,1024]{1,0:T(8,128)(2,1)} %latent_proj.3) | copy-start | bytes 6291460
  55.8 7.8 %copy-start.3 = (f32[256,1024]{1,0:T(8,128)S(1)}, f32[256,1024]{1,0:T(8,128)}, u32[]{:S(2)}) copy-start(f32[256,1024]{1,0:T(8,128)} %get-tuple-element.17.before) | copy-start | bytes 3145732
  63.0 2.4 %collective-permute-start = (bf16[2,512,256]{2,1,0:T(8,128)(2,1)S(1)}, bf16[2,512,256]{2,1,0:T(8,128)(2,1)S(1)}, u32[]{:S(2)}, u32[]{:S(2)}) collective-permute-start(bf16[2,512,256]{2,1,0:T(8,128)(2,1)S(1)} %get-tuple-element.15), channel_id=1, source_target_pairs={{0,2},{2,0},{1,3},{3,1},{4,6},{6,4},{5,7},{7,5},{8,10},{10,8},{9,1... | collective-permute-start | bytes 1572872 | tf_op jit(solution)/shard_map/ppermute | solution.py:329
  63.3 2.5 %collective-permute-start.2 = (bf16[256,1024]{1,0:T(8,128)(2,1)S(1)}, bf16[256,1024]{1,0:T(8,128)(2,1)S(1)}, u32[]{:S(2)}, u32[]{:S(2)}) collective-permute-start(bf16[256,1024]{1,0:T(8,128)(2,1)S(1)} %back.1.dlatent.grad_own), channel_id=1, source_target_pairs={{0,2},{2,0},{1,3},{3,1},{4,6},{6,4},{5,7},{7,5},{8,10},{10,8},{9,1... | collective-permute-start | bytes 1572872 | tf_op jit(solution)/shard_map/ppermute | solution.py:330
  65.1 2.0 %collective-permute-start.1 = (bf16[256,1024]{1,0:T(8,128)(2,1)S(1)}, bf16[256,1024]{1,0:T(8,128)(2,1)S(1)}, u32[]{:S(2)}, u32[]{:S(2)}) collective-permute-start(bf16[256,1024]{1,0:T(8,128)(2,1)S(1)} %token_.1.grad_own), channel_id=1, source_target_pairs={{0,2},{2,0},{1,3},{3,1},{4,6},{6,4},{5,7},{7,5},{8,10},{10,8},{9,1... | collective-permute-start | bytes 1572872 | tf_op jit(solution)/shard_map/ppermute | solution.py:341

commit v5 on v4

--- a/solution.py
+++ b/solution.py
@@ -254,7 +254,7 @@
 
 UNIT = 2 * TOK * D * D
 MIB = 1 << 20
-FRONT_LIMIT = 52 * MIB
+FRONT_LIMIT = 50 * MIB
 TIME_LIMIT = 28 * MIB
 
 

time: 108 us -> 106 us (0.981)
  no operation moved by 1% of the time
where the time goes in v5:
time: 106 us
  blocking collectives  73.9 us (70%)
  Pallas kernels  28.9 us (27%)
    all_to_all x3, blocking collectives, exchange(): return lax.all_to_all(values, axes, split_axis=0, concat_axis=0, tiled=True)  73.9 us
    pallas_call x7, Pallas kernels, call(): pl.pallas_call(kernel, out_shape=outs, in_specs=in_specs, out_specs=out_s...  28.9 us
  transfers between devices with their start and end apart: 3, of which 2 were waited for; matrix products, arithmetic and copies ran while one was open for 0% of the time, Pallas kernels for 2%

profile of v5, /device:TPU:0, one launch (start us, length us, event | category | flops | bytes accessed | tf_op | source)
XLA Modules:
  0.0 106.3 jit_solution(18240005178868688783)
XLA Ops:
  0.6 0.7 pad_maximum_fusion.gains
  1.4 0.0 copy-start.3
  1.4 9.0 %front.1 = (bf16[2,512,256]{2,1,0:T(8,128)(2,1)S(1)}, bf16[2,512,256]{2,1,0:T(8,128)(2,1)S(1)}, f32[256,1024]{1,0:T(8,128)S(1)}, bf16[256,1024]{1,0:T(8,128)(2,1...) custom-call(s32[256,1024]{1,0:T(8,128)} %bitcast.11, bf16[2,16,16,1024]{3,2,1,0:T(8,128)(2,1)} %bitcast.12, ...), custom_call_target="tpu_custom_call" | custom-call | flops 4294967296 | bytes 20971520 | tf_op jit(solution)/shard_map/front/pallas_call | solution.py:241
  10.4 0.0 copy-start.4
  10.4 0.0 copy-start.6
  10.4 0.0 slice-start
  10.4 22.1 %all_to_all.21.packed = bf16[16,2,16,1024]{3,2,1,0:T(8,128)(2,1)S(1)} all-to-all(bf16[16,2,16,1024]{3,2,1,0:T(8,128)(2,1)S(1)} %get-tuple-element.11), channel_id=1, replica_groups=mesh['grp'=2,'x'=4,'z'=4,'core'=2,'dp'=2] {'z','core','grp'}, dimensions={0} | all-to-all | bytes 2097152 | tf_op jit(solution)/shard_map/all_to_all | solution.py:282
  32.5 0.0 slice-start.1
  32.6 0.0 copy-start.1
  32.6 0.0 copy-start.2
  32.6 8.9 %time.1 = bf16[256,1024]{1,0:T(8,128)(2,1)S(1)} custom-call(s32[2,4]{1,0:T(2,128)S(1)} %copy-done.6, bf16[16,2,16,1024]{3,2,1,0:T(8,128)(2,1)S(1)} %all_to_all.21.packed, f32[3,1024]{1,0:T(4,128)S(1)} %pad_maximum_fusion.gains, bf16[1024,3072]{1,0:T(8,128)(2,1)S(1)} %copy-done.3, bf16[1024,1024]{1,0:T(8,128)(2,1)S(1)} %copy-done.4), custom_call_target="tpu_custom_call" | custom-call | flops 4831838208 | bytes 10485760 | tf_op jit(solution)/shard_map/time/pallas_call | solution.py:241
  41.5 13.2 %all_to_all.22 = bf16[16,16,1024]{2,1,0:T(8,128)(2,1)S(1)} all-to-all(bf16[16,16,1024]{2,1,0:T(8,128)(2,1)S(1)} %bitcast.10), channel_id=1, replica_groups=mesh['grp'=2,'x'=4,'z'=4,'core'=2,'dp'=2] {'z','core','grp'}, dimensions={0} | all-to-all | bytes 1048576 | tf_op jit(solution)/shard_map/all_to_all | solution.py:282
  54.8 0.0 copy-start
  54.8 7.2 %back.1.dlatent.grad_own = bf16[256,1024]{1,0:T(8,128)(2,1)S(1)} custom-call(bf16[256,1024]{1,0:T(8,128)(2,1)S(1)} %bitcast.9, bf16[256,3072]{1,0:T(8,128)(2,1)S(1)} %copy-done.5, bf16[256,1024]{1,0:T(8,128)(2,1)S(1)} %get-tuple-element.13.stream, f32[3,1024]{1,0:T(4,128)S(1)} %pad_maximum_fusion.gains, bf16[1024,1024]{1,0:T(8,128)(2,1)S(1)} %copy-done.2, ...), custom_call_target="tpu_custom_call" | custom-call | flops 3758096384 | bytes 14680064 | tf_op jit(solution)/shard_map/back/pallas_call | solution.py:241
  62.0 0.2 collective-permute-start
  62.2 0.3 collective-permute-start.2
  62.6 1.5 %token_.1.grad_own = bf16[256,1024]{1,0:T(8,128)(2,1)S(1)} custom-call(bf16[256,1024]{1,0:T(8,128)(2,1)S(1)} %back.1.dlatent.grad_own, f32[256,1024]{1,0:T(8,128)S(1)} %get-tuple-element.17.before, f32[3,1024]{1,0:T(4,128)S(1)} %pad_maximum_fusion.gains, bf16[1024,1024]{1,0:T(8,128)(2,1)S(1)} %copy-done), custom_call_target="tpu_custom_call" | custom-call | flops 536870912 | bytes 4194304 | tf_op jit(solution)/shard_map/token/pallas_call | solution.py:241
  64.1 0.2 collective-permute-start.1
  64.3 0.4 collective-permute-done.2.grad_other
  64.7 0.7 latent_weight.1.latent
  65.4 0.6 collective-permute-done.1.grad_other
  66.1 0.7 pillar_weight.1
  66.8 38.6 %all_to_all.23.parts = bf16[64,2,8,1024]{3,2,1,0:T(8,128)(2,1)S(1)} all-to-all(bf16[64,2,8,1024]{3,2,1,0:T(8,128)(2,1)S(1)} %pillar_weight.1), channel_id=1, replica_groups=mesh['grp'=2,'x'=4,'z'=4,'core'=2,'dp'=2] {'grp','x','z','dp'}, dimensions={0} | all-to-all | bytes 4194304 | tf_op jit(solution)/shard_map/all_to_all | solution.py:282
  105.3 0.9 total.1
  (12 shorter events, 0.0 us)
Async XLA Ops:
  1.4 31.2 %copy-start.3 = (bf16[1024,3072]{1,0:T(8,128)(2,1)S(1)}, bf16[1024,3072]{1,0:T(8,128)(2,1)}, u32[]{:S(2)}) copy-start(bf16[1024,3072]{1,0:T(8,128)(2,1)} %w_project.2) | copy-start | bytes 18874372
  10.4 22.1 %copy-start.4 = (bf16[1024,1024]{1,0:T(8,128)(2,1)S(1)}, bf16[1024,1024]{1,0:T(8,128)(2,1)}, u32[]{:S(2)}) copy-start(bf16[1024,1024]{1,0:T(8,128)(2,1)} %w_output.2) | copy-start | bytes 6291460
  10.4 22.1 %copy-start.6 = (s32[2,4]{1,0:T(2,128)S(1)}, s32[2,4]{1,0:T(2,128)}, u32[]{:S(2)}) copy-start(s32[2,4]{1,0:T(2,128)} %valid_frames.1) | copy-start | bytes 100
  10.4 44.3 %slice-start = ((s8[6291456]{0:T(1024)(128)(4,1)}), s8[4194304]{0:T(1024)(128)(4,1)S(1)}, s32[]{:S(2)}) async-start(s8[6291456]{0:T(1024)(128)(4,1)} %bitcast.7), calls=%async_computation.3 | async-start | bytes 8388608
  32.5 22.2 %slice-start.1 = ((s8[6291456]{0:T(1024)(128)(4,1)}), s8[2097152]{0:T(1024)(128)(4,1)S(1)}, s32[]{:S(2)}) async-start(s8[6291456]{0:T(1024)(128)(4,1)} %bitcast.7), calls=%async_computation.4 | async-start | bytes 4194304
  32.6 22.2 %copy-start.1 = (bf16[1024,1024]{1,0:T(8,128)(2,1)S(1)}, bf16[1024,1024]{1,0:T(8,128)(2,1)}, u32[]{:S(2)}) copy-start(bf16[1024,1024]{1,0:T(8,128)(2,1)} %w_input.1) | copy-start | bytes 6291460
  32.6 22.2 %copy-start.2 = (bf16[1024,1024]{1,0:T(8,128)(2,1)S(1)}, bf16[1024,1024]{1,0:T(8,128)(2,1)}, u32[]{:S(2)}) copy-start(bf16[1024,1024]{1,0:T(8,128)(2,1)} %w_output.3) | copy-start | bytes 6291460
  32.6 22.2 %copy-start.5 = (bf16[256,3072]{1,0:T(8,128)(2,1)S(1)}, bf16[256,3072]{1,0:T(8,128)(2,1)}, u32[]{:S(2)}) copy-start(bf16[256,3072]{1,0:T(8,128)(2,1)} %get-tuple-element.12.joined) | copy-start | bytes 4718596
  54.8 7.8 %copy-start = (bf16[1024,1024]{1,0:T(8,128)(2,1)S(1)}, bf16[1024,1024]{1,0:T(8,128)(2,1)}, u32[]{:S(2)}) copy-start(bf16[1024,1024]{1,0:T(8,128)(2,1)} %latent_proj.3) | copy-start | bytes 6291460
  62.0 2.3 %collective-permute-start = (bf16[2,512,256]{2,1,0:T(8,128)(2,1)S(1)}, bf16[2,512,256]{2,1,0:T(8,128)(2,1)S(1)}, u32[]{:S(2)}, u32[]{:S(2)}) collective-permute-start(bf16[2,512,256]{2,1,0:T(8,128)(2,1)S(1)} %get-tuple-element.15), channel_id=1, source_target_pairs={{0,2},{2,0},{1,3},{3,1},{4,6},{6,4},{5,7},{7,5},{8,10},{10,8},{9,1... | collective-permute-start | bytes 1572872 | tf_op jit(solution)/shard_map/ppermute | solution.py:329
  62.2 2.5 %collective-permute-start.2 = (bf16[256,1024]{1,0:T(8,128)(2,1)S(1)}, bf16[256,1024]{1,0:T(8,128)(2,1)S(1)}, u32[]{:S(2)}, u32[]{:S(2)}) collective-permute-start(bf16[256,1024]{1,0:T(8,128)(2,1)S(1)} %back.1.dlatent.grad_own), channel_id=1, source_target_pairs={{0,2},{2,0},{1,3},{3,1},{4,6},{6,4},{5,7},{7,5},{8,10},{10,8},{9,1... | collective-permute-start | bytes 1572872 | tf_op jit(solution)/shard_map/ppermute | solution.py:330
  64.1 2.0 %collective-permute-start.1 = (bf16[256,1024]{1,0:T(8,128)(2,1)S(1)}, bf16[256,1024]{1,0:T(8,128)(2,1)S(1)}, u32[]{:S(2)}, u32[]{:S(2)}) collective-permute-start(bf16[256,1024]{1,0:T(8,128)(2,1)S(1)} %token_.1.grad_own), channel_id=1, source_target_pairs={{0,2},{2,0},{1,3},{3,1},{4,6},{6,4},{5,7},{7,5},{8,10},{10,8},{9,1... | collective-permute-start | bytes 1572872 | tf_op jit(solution)/shard_map/ppermute | solution.py:341
